TPU v7x, 512 devices: a whole 4x8x8 slice. The times are simulated.
512 devices in a mesh: layer: 16 (over z, core), plane: 32 (over x, y).
Axes of the slice: x: 4, y: 8, z: 8, core: 2. Of those that a mesh axis runs over, the one named last changes fastest.
Arguments:
- velocity: bfloat16 [2, 128, 131072], P(None, 'layer', 'plane'), may hold values from -6 to 6
- adjoint: bfloat16 [2, 128, 131072], P(None, 'layer', 'plane'), may hold values from -6 to 6
- corners: int32 [4, 131072], P(None, 'plane'), may hold values from 0 to 4607, as said below
- shared: int32 [4, 4096], P(None, 'plane'), may hold values from 0 to 4096, as said below
- stretch: float32 [2, 131072], P(None, 'plane'), may hold values from 0.5 to 2
- shear_part: float32 [2, 131072], P(None, 'plane'), may hold values from -0.2 to 0.2
- thickness: float32 [128, 131072], P('layer', 'plane'), may hold values from 0.3 to 3
- rate_factor: float32 [128, 131072], P('layer', 'plane'), may hold values from 0.5 to 2
- retention: float32 [128, 131072], P('layer', 'plane'), may hold values from 0.2 to 1
- weight: float32 [128, 131072], P('layer', 'plane'), may hold values from 0.5 to 2
Outputs:
- gradient: float32 [131072], P('plane')
Inputs may be any that keep to these rules, and one draw needn't show every extreme that they name: `corners`: below 4096 a number names an owned node; 4096 + j * 128 + s names slot s of the ghost block of direction j (plane offsets -2, -1, +1, +2). Every slot of a block whose partition exists is named by exactly one corner, corner 0 of some element; blocks of directions beyond the ends of the plane axis are named by none. `shared`: row j, block p lists 128 distinct owned nodes of partition p that the partition at offset o_j (-2, -1, +1, +2) holds as ghosts; the block is 4096 throughout where that partition does not exist.
All inputs are finite; a program needn't handle non-finite values.
Results may differ from a plain program's by a relative error of at most 0.0003.
Values may be sent and summed in bfloat16 or wider, within the bound.
A program may use at most 128 MiB of HBM per device.

v0:
```python
import math

import jax
import jax.numpy as jnp
from jax import lax
from jax.sharding import PartitionSpec as P

OFFSETS = (-2, -1, 1, 2)
STRAIN_EPS = 0.01
LOW_SPAN = 64


def shifted(value, axis, steps):
    count = lax.axis_size(axis)
    first, last = (max(0, -steps), min(count, count - steps))
    return lax.ppermute(value, axis, [(source, source + steps) for source in range(first, last)])


def entering_2(value, axis, combine, identity):
    devices, place = (lax.axis_size(axis), lax.axis_index(axis))
    everything = jax.tree.map(lambda part: lax.all_gather(part, axis), value)
    start = jax.tree.map(
        lambda part, zero: jnp.broadcast_to(jnp.asarray(zero, part.dtype), part.shape),
        value,
        identity,
    )

    def hop(k, before):
        reached = k < place
        new = combine(before, jax.tree.map(lambda part: part[k], everything))
        return jax.tree.map(lambda a, b: jnp.where(reached, a, b), new, before)

    return lax.fori_loop(0, devices, hop, start)


def basis_table():
    gauss_point = 1.0 / math.sqrt(3.0)
    xi_signs = [-1.0, 1.0, 1.0, -1.0, -1.0, 1.0, 1.0, -1.0]
    eta_signs = [-1.0, -1.0, 1.0, 1.0, -1.0, -1.0, 1.0, 1.0]
    zeta_signs = [1.0, 1.0, 1.0, 1.0, -1.0, -1.0, -1.0, -1.0]
    shape_table = [[0.0] * 8 for row_index in range(24)]
    for point_index in range(8):
        xi_point = gauss_point if point_index & 1 else -gauss_point
        eta_point = gauss_point if point_index & 2 else -gauss_point
        zeta_point = gauss_point if point_index & 4 else -gauss_point
        for node_index in range(8):
            along_xi = 1.0 + xi_signs[node_index] * xi_point
            along_eta = 1.0 + eta_signs[node_index] * eta_point
            along_zeta = 1.0 + zeta_signs[node_index] * zeta_point
            shape_table[point_index][node_index] = (
                xi_signs[node_index] * along_eta * along_zeta / 8.0
            )
            shape_table[8 + point_index][node_index] = (
                eta_signs[node_index] * along_xi * along_zeta / 8.0
            )
            shape_table[16 + point_index][node_index] = (
                zeta_signs[node_index] * along_xi * along_eta / 8.0
            )
    return shape_table


def strain_of(grad_x, grad_y, grad_z, first_comp, second_comp):
    return (
        grad_x[first_comp],
        grad_y[second_comp],
        0.5 * (grad_y[first_comp] + grad_x[second_comp]),
        0.5 * grad_z[first_comp],
        0.5 * grad_z[second_comp],
    )


def pairing(left_strain, right_strain):
    return (
        left_strain[0] * right_strain[0]
        + left_strain[1] * right_strain[1]
        + 0.5 * (left_strain[0] * right_strain[1] + left_strain[1] * right_strain[0])
        + left_strain[2] * right_strain[2]
        + left_strain[3] * right_strain[3]
        + left_strain[4] * right_strain[4]
    )


def element_terms(nodal_values, stretch, shear_part, thickness, rate_factor):
    layer_count = nodal_values.shape[1] - 1
    width = nodal_values.shape[3]
    top_nodes = nodal_values[:, :-1]
    bottom_nodes = nodal_values[:, 1:]
    hexa_nodes = jnp.concatenate([top_nodes, bottom_nodes], axis=2)
    basis = jnp.asarray(basis_table(), dtype=jnp.float32)
    derived = jnp.einsum("rn,clnb->clrb", basis, hexa_nodes, precision=lax.Precision.HIGHEST)
    derived = derived.reshape(4, layer_count, 3, 8, width)
    along_xi = derived[:, :, 0]
    along_eta = derived[:, :, 1]
    along_zeta = derived[:, :, 2]
    grad_x = stretch[0] * along_xi + shear_part[0] * along_eta
    grad_y = shear_part[1] * along_xi + stretch[1] * along_eta
    grad_z = (2.0 / thickness)[None, :, None, :] * along_zeta
    flow_strain = strain_of(grad_x, grad_y, grad_z, 0, 1)
    adjoint_strain = strain_of(grad_x, grad_y, grad_z, 2, 3)
    effective = pairing(flow_strain, flow_strain) + STRAIN_EPS
    viscosity = 0.5 * rate_factor[:, None, :] * jnp.power(effective, -1.0 / 3.0)
    volume = 0.5 * thickness / (stretch[0] * stretch[1] - shear_part[0] * shear_part[1])
    return volume * jnp.sum(4.0 * viscosity * pairing(flow_strain, adjoint_strain), axis=1)


def high_select(node_ids, high_count, dtype):
    high_part = node_ids // LOW_SPAN
    return (jnp.arange(high_count, dtype=jnp.int32)[:, None] == high_part[None, :]).astype(dtype)


def low_select(node_ids):
    low_part = node_ids % LOW_SPAN
    return (jnp.arange(LOW_SPAN, dtype=jnp.int32)[:, None] == low_part[None, :]).astype(jnp.float32)


def compose(earlier, later):
    return (earlier[0] * later[0], later[0] * earlier[1] + later[1])


def shards(
    velocity,
    adjoint,
    corners,
    shared,
    stretch,
    shear_part,
    thickness,
    rate_factor,
    retention,
    weight,
):
    owned_count = velocity.shape[2]
    layer_count = velocity.shape[1]
    slot_count = shared.shape[1]
    elem_count = corners.shape[1]
    fields = jnp.concatenate([velocity, adjoint], axis=0)
    padded = jnp.concatenate([fields, jnp.zeros((4, layer_count, 1), fields.dtype)], axis=2)
    outgoing = [jnp.take(padded, shared[direction], axis=2) for direction in range(4)]
    incoming = [
        shifted(outgoing[3 - direction], "plane", -OFFSETS[direction]) for direction in range(4)
    ]
    local_fields = jnp.concatenate([fields] + incoming, axis=2)
    local_count = local_fields.shape[2]
    high_count = local_count // LOW_SPAN
    below_level = shifted(local_fields[:, 0], "layer", -1)
    levels = jnp.concatenate([local_fields, below_level[:, None]], axis=1)
    level_rows = 4 * (layer_count + 1)
    level_table = levels.reshape(level_rows, high_count, LOW_SPAN)
    level_table = jnp.transpose(level_table, (0, 2, 1)).reshape(level_rows * LOW_SPAN, high_count)
    block_size = min(1024, elem_count)
    block_count = elem_count // block_size

    def one_block(block_start):
        corner_ids = lax.dynamic_slice_in_dim(corners, block_start, block_size, 1).reshape(-1)
        picked = jnp.dot(
            level_table,
            high_select(corner_ids, high_count, jnp.bfloat16),
            preferred_element_type=jnp.float32,
        )
        picked = picked.reshape(level_rows, LOW_SPAN, 4 * block_size)
        nodal_values = jnp.sum(picked * low_select(corner_ids)[None], axis=1)
        nodal_values = nodal_values.reshape(4, layer_count + 1, 4, block_size)
        return element_terms(
            nodal_values,
            lax.dynamic_slice_in_dim(stretch, block_start, block_size, 1),
            lax.dynamic_slice_in_dim(shear_part, block_start, block_size, 1),
            lax.dynamic_slice_in_dim(thickness, block_start, block_size, 1),
            lax.dynamic_slice_in_dim(rate_factor, block_start, block_size, 1),
        )

    layer_terms = lax.map(one_block, jnp.arange(block_count, dtype=jnp.int32) * block_size)
    layer_terms = jnp.transpose(layer_terms, (1, 0, 2)).reshape(layer_count, elem_count)
    factor = jnp.ones((elem_count,), jnp.float32)
    offset = jnp.zeros((elem_count,), jnp.float32)
    for layer_index in range(layer_count):
        factor = retention[layer_index] * factor
        offset = (
            retention[layer_index] * offset + (1.0 - retention[layer_index]) * weight[layer_index]
        )
    identity = (jnp.ones((elem_count,), jnp.float32), jnp.zeros((elem_count,), jnp.float32))
    _, entering = entering_2((factor, offset), "layer", compose, identity)
    running = entering
    column = jnp.zeros((elem_count,), jnp.float32)
    for layer_index in range(layer_count):
        running = (
            retention[layer_index] * running + (1.0 - retention[layer_index]) * weight[layer_index]
        )
        column = column + running * layer_terms[layer_index]
    quarter = 0.25 * column

    def add_block(block_index, node_table):
        block_start = block_index * block_size
        corner_ids = lax.dynamic_slice_in_dim(corners, block_start, block_size, 1).reshape(-1)
        values = jnp.tile(lax.dynamic_slice_in_dim(quarter, block_start, block_size, 0), 4)
        low_values = low_select(corner_ids) * values[None, :]
        return node_table + jnp.dot(
            low_values,
            high_select(corner_ids, high_count, jnp.float32).T,
            precision=lax.Precision.HIGHEST,
            preferred_element_type=jnp.float32,
        )

    node_table = lax.fori_loop(
        0, block_count, add_block, jnp.zeros((LOW_SPAN, high_count), jnp.float32)
    )
    partial_nodes = jnp.transpose(node_table).reshape(local_count)
    summed = lax.psum(partial_nodes, "layer")
    ghost_part = summed[owned_count:].reshape(4, slot_count)
    arriving = [
        shifted(ghost_part[3 - direction], "plane", -OFFSETS[direction]) for direction in range(4)
    ]
    owned_sum = jnp.concatenate([summed[:owned_count], jnp.zeros((1,), jnp.float32)])
    for direction in range(4):
        owned_sum = owned_sum.at[shared[direction]].add(arriving[direction])
    return owned_sum[:owned_count]


def solution(mesh):
    return jax.shard_map(
        shards,
        mesh=mesh,
        in_specs=(
            P(None, "layer", "plane"),
            P(None, "layer", "plane"),
            P(None, "plane"),
            P(None, "plane"),
            P(None, "plane"),
            P(None, "plane"),
            P("layer", "plane"),
            P("layer", "plane"),
            P("layer", "plane"),
            P("layer", "plane"),
        ),
        out_specs=P("plane"),
        check_vma=False,
    )
```

profile of v0, /device:TPU:7, one launch (start us, length us, event | category | flops | bytes accessed | tf_op | source)
XLA Modules:
  0.0 328.3 jit_solution(698319157925830426)
XLA Ops:
  0.0 0.8 compare_and_fusion
  0.9 1.0 pad_maximum_fusion.1
  1.9 4.6 %copy.48 = bf16[4,8,4096]{1,0,2:T(4,128)(2,1)} copy(bf16[4,8,4096]{2,1,0:T(8,128)(2,1)S(1)} %pad_maximum_fusion.1) | data formatting | bytes 524288 | tf_op jit(solution)/shard_map/concatenate | solution.py:136
  6.5 6.8 %concatenate.22 = bf16[4,8,4097]{1,0,2:T(4,128)(2,1)} pad(bf16[4,8,4096]{1,0,2:T(4,128)(2,1)} %copy.48, bf16[]{:T(256)} %constant.242.clone.1), padding=0_0x0_0x0_1 | pad | bytes 524354 | tf_op jit(solution)/shard_map/concatenate | solution.py:137
  13.3 3.0 gather_fusion
  16.5 4.2 %collective-permute-start = (bf16[4,8,128]{1,0,2:T(4,128)(2,1)S(1)}, bf16[4,8,128]{1,0,2:T(4,128)(2,1)S(1)}, u32[]{:S(2)}, u32[]{:S(2)}) collective-permute-start(bf16[4,8,128]{1,0,2:T(4,128)(2,1)S(1)} %select_bitcast_fusion.3), channel_id=1, source_target_pairs={{0,2},{1,3},{2,4},{3,5},{4,6},{5,7},{6,8},{7,9},{8,10},{9,11},{10,... | collective-permute-start | bytes 24584 | tf_op jit(solution)/shard_map/ppermute | solution.py:16
  20.7 2.9 gather_fusion.1
  23.9 3.2 collective-permute-start.1
  27.1 2.9 gather_fusion.2
  30.3 4.2 %collective-permute-start.2 = (bf16[4,8,128]{1,0,2:T(4,128)(2,1)S(1)}, bf16[4,8,128]{1,0,2:T(4,128)(2,1)S(1)}, u32[]{:S(2)}, u32[]{:S(2)}) collective-permute-start(bf16[4,8,128]{1,0,2:T(4,128)(2,1)S(1)} %select_bitcast_fusion.1), channel_id=1, source_target_pairs={{1,0},{2,1},{3,2},{4,3},{5,4},{6,5},{7,6},{8,7},{9,8},{10,9},{11,1... | collective-permute-start | bytes 24584 | tf_op jit(solution)/shard_map/ppermute | solution.py:16
  34.5 2.9 gather_fusion.3
  37.7 2.1 collective-permute-start.3
  39.8 0.7 multiply_bitcast_fusion
  40.5 0.9 add_bitcast_fusion
  41.4 0.7 fusion.40
  42.1 25.5 %all-gather = f32[16,1,4096]{2,1,0:T(1,128)S(1)} all-gather(f32[1,1,4096]{2,1,0:T(1,128)S(1)} %get-tuple-element.500), channel_id=1, replica_groups=mesh['layer'=16,'plane'=32] {'layer'}, dimensions={0}, use_global_device_ids=true | all-gather | bytes 278528 | tf_op jit(solution)/shard_map/all_gather | solution.py:21
  67.8 15.2 %all-gather.1 = f32[16,1,4096]{2,1,0:T(1,128)S(1)} all-gather(f32[1,1,4096]{2,1,0:T(1,128)S(1)} %get-tuple-element.496), channel_id=1, replica_groups=mesh['layer'=16,'plane'=32] {'layer'}, dimensions={0}, use_global_device_ids=true | all-gather | bytes 278528 | tf_op jit(solution)/shard_map/all_gather | solution.py:21
  83.1 1.2 while.44
  85.5 2.3 collective-permute-start.4
  87.8 3.0 collective-permute-done.4
  91.4 1.1 copy.58
  92.5 163.1 %while.43 = (s32[]{:T(128)}, f32[4,8,1024]{2,1,0:T(8,128)S(1)}, s32[4]{0:T(128)S(1)}, f32[8,4096]{1,0:T(8,128)S(1)}, f32[2,4096]{1,0:T(2,128)}, /*index=5*/f32[2...) while((s32[]{:T(128)}, f32[4,8,1024]{2,1,0:T(8,128)S(1)}, ...), condition=%wide.region_5.7_spmd.clone, body=%wide.region_2.6_spmd.sunk.clone.sunk | while | flops 1458830336 | bytes 95925216 | solution.py:171
  92.5 0.6 dynamic_slice.104
  95.1 16.0 %fusion.57 = f32[4096,2304]{0,1:T(8,128)} fusion(bf16[2304,72]{1,0:T(8,128)(2,1)} %get-tuple-element.719, s32[4096]{0:T(1024)S(1)} %get-tuple-element.656), kind=kOutput, calls=%fused_computation.11.clone.1 | convolution fusion | flops 1359249408 | bytes 38096896 | tf_op jit(solution)/shard_map/while/body/eval_jaxpr/dot_general | solution.py:155
  111.2 14.8 %multiply_reduce_fusion.2 = f32[36,4096]{1,0:T(8,128)S(1)} fusion(f32[36,64,4096]{2,1,0:T(8,128)} %bitcast.239, f32[64,4096]{1,0:T(8,128)S(1)} %fusion.58), kind=kLoop, calls=%fused_computation.8.clone.1 | loop fusion | flops 18726912 | bytes 39387136 | tf_op jit(solution)/shard_map/while/body/eval_jaxpr/reduce_sum | solution.py:161
  126.6 3.6 %convolution_bitcast_fusion.2 = f32[4,8,3,8,1024]{4,3,2,1,0:T(8,128)S(1)} fusion(f32[24,8,1,1]{0,1,3,2:T(8,128)S(1)} %get-tuple-element.721, f32[4,8,4,1024]{3,2,1,0:T(4,128)S(1)} %get-tuple-element.658, f32[4,8,4,1024]{3,2,1,0:T(4,128)S(1)} %get-tuple-element.659), kind=kOutput, calls=%fused_computation.9.clone.1 | convolution fusion | flops 75759616 | bytes 4195072 | tf_op jit(solution)/shard_map/while/body/eval_jaxpr/rn,clnb->clrb/dot_general | solution.py:90
  130.3 0.9 multiply_subtract_fusion.2
  131.2 0.9 dynamic-slice_multiply_fusion.2
  132.5 0.7 fusion.60
  133.3 0.6 dynamic_slice.104
  135.9 16.0 %fusion.57 = f32[4096,2304]{0,1:T(8,128)} fusion(bf16[2304,72]{1,0:T(8,128)(2,1)} %get-tuple-element.719, s32[4096]{0:T(1024)S(1)} %get-tuple-element.656), kind=kOutput, calls=%fused_computation.11.clone.1 | convolution fusion | flops 1359249408 | bytes 38096896 | tf_op jit(solution)/shard_map/while/body/eval_jaxpr/dot_general | solution.py:155
  152.0 14.8 %multiply_reduce_fusion.2 = f32[36,4096]{1,0:T(8,128)S(1)} fusion(f32[36,64,4096]{2,1,0:T(8,128)} %bitcast.239, f32[64,4096]{1,0:T(8,128)S(1)} %fusion.58), kind=kLoop, calls=%fused_computation.8.clone.1 | loop fusion | flops 18726912 | bytes 39387136 | tf_op jit(solution)/shard_map/while/body/eval_jaxpr/reduce_sum | solution.py:161
  167.4 3.6 %convolution_bitcast_fusion.2 = f32[4,8,3,8,1024]{4,3,2,1,0:T(8,128)S(1)} fusion(f32[24,8,1,1]{0,1,3,2:T(8,128)S(1)} %get-tuple-element.721, f32[4,8,4,1024]{3,2,1,0:T(4,128)S(1)} %get-tuple-element.658, f32[4,8,4,1024]{3,2,1,0:T(4,128)S(1)} %get-tuple-element.659), kind=kOutput, calls=%fused_computation.9.clone.1 | convolution fusion | flops 75759616 | bytes 4195072 | tf_op jit(solution)/shard_map/while/body/eval_jaxpr/rn,clnb->clrb/dot_general | solution.py:90
  171.1 0.9 multiply_subtract_fusion.2
  172.0 0.9 dynamic-slice_multiply_fusion.2
  173.3 0.7 fusion.60
  176.7 16.0 %fusion.57 = f32[4096,2304]{0,1:T(8,128)} fusion(bf16[2304,72]{1,0:T(8,128)(2,1)} %get-tuple-element.719, s32[4096]{0:T(1024)S(1)} %get-tuple-element.656), kind=kOutput, calls=%fused_computation.11.clone.1 | convolution fusion | flops 1359249408 | bytes 38096896 | tf_op jit(solution)/shard_map/while/body/eval_jaxpr/dot_general | solution.py:155
  192.8 14.8 %multiply_reduce_fusion.2 = f32[36,4096]{1,0:T(8,128)S(1)} fusion(f32[36,64,4096]{2,1,0:T(8,128)} %bitcast.239, f32[64,4096]{1,0:T(8,128)S(1)} %fusion.58), kind=kLoop, calls=%fused_computation.8.clone.1 | loop fusion | flops 18726912 | bytes 39387136 | tf_op jit(solution)/shard_map/while/body/eval_jaxpr/reduce_sum | solution.py:161
  208.2 3.6 %convolution_bitcast_fusion.2 = f32[4,8,3,8,1024]{4,3,2,1,0:T(8,128)S(1)} fusion(f32[24,8,1,1]{0,1,3,2:T(8,128)S(1)} %get-tuple-element.721, f32[4,8,4,1024]{3,2,1,0:T(4,128)S(1)} %get-tuple-element.658, f32[4,8,4,1024]{3,2,1,0:T(4,128)S(1)} %get-tuple-element.659), kind=kOutput, calls=%fused_computation.9.clone.1 | convolution fusion | flops 75759616 | bytes 4195072 | tf_op jit(solution)/shard_map/while/body/eval_jaxpr/rn,clnb->clrb/dot_general | solution.py:90
  211.8 0.9 multiply_subtract_fusion.2
  212.7 0.9 dynamic-slice_multiply_fusion.2
  214.1 0.7 fusion.60
  217.5 16.0 %fusion.57 = f32[4096,2304]{0,1:T(8,128)} fusion(bf16[2304,72]{1,0:T(8,128)(2,1)} %get-tuple-element.719, s32[4096]{0:T(1024)S(1)} %get-tuple-element.656), kind=kOutput, calls=%fused_computation.11.clone.1 | convolution fusion | flops 1359249408 | bytes 38096896 | tf_op jit(solution)/shard_map/while/body/eval_jaxpr/dot_general | solution.py:155
  233.5 14.8 %multiply_reduce_fusion.2 = f32[36,4096]{1,0:T(8,128)S(1)} fusion(f32[36,64,4096]{2,1,0:T(8,128)} %bitcast.239, f32[64,4096]{1,0:T(8,128)S(1)} %fusion.58), kind=kLoop, calls=%fused_computation.8.clone.1 | loop fusion | flops 18726912 | bytes 39387136 | tf_op jit(solution)/shard_map/while/body/eval_jaxpr/reduce_sum | solution.py:161
  249.0 3.6 %convolution_bitcast_fusion.2 = f32[4,8,3,8,1024]{4,3,2,1,0:T(8,128)S(1)} fusion(f32[24,8,1,1]{0,1,3,2:T(8,128)S(1)} %get-tuple-element.721, f32[4,8,4,1024]{3,2,1,0:T(4,128)S(1)} %get-tuple-element.658, f32[4,8,4,1024]{3,2,1,0:T(4,128)S(1)} %get-tuple-element.659), kind=kOutput, calls=%fused_computation.9.clone.1 | convolution fusion | flops 75759616 | bytes 4195072 | tf_op jit(solution)/shard_map/while/body/eval_jaxpr/rn,clnb->clrb/dot_general | solution.py:90
  252.6 0.9 multiply_subtract_fusion.2
  253.5 0.9 dynamic-slice_multiply_fusion.2
  254.8 0.7 fusion.60
  255.8 0.9 add_multiply_fusion
  256.7 8.7 %while.45 = (s32[]{:T(128)}, f32[64,72]{1,0:T(8,128)}, s32[4,4096]{1,0:T(4,128)S(1)}, f32[4096]{0:T(1024)S(1)}, s32[]{:T(128)}, /*index=5*/s32[]{:T(128)}, s32[]{:T(128)}, s32[]{:T(128)}) while((s32[]{:T(128)}, f32[64,72]{1,0:T(8,128)}, s32[4,4096]{1,0:T(4,128)S(1)}, f32[4096]{0:T(1024)S(1)}, s32[]{:T(128)}, /*index=5*/s32[]{:T(128)}, ...), condition=%wide.region_7.9_spmd.clone, body=%wide.region_6.8_spmd.clone.sunk | while | flops 227398656 | bytes 229525 | solution.py:203
  256.8 1.5 fusion.62
  258.4 2.3 fusion.62
  260.8 2.3 fusion.62
  263.2 2.3 fusion.62
  265.4 0.8 copy.56
  266.3 42.5 %psum.7 = f32[4608]{0:T(1024)S(1)} all-reduce(f32[4608]{0:T(1024)S(1)} %reshape.352), channel_id=1, replica_groups=mesh['layer'=16,'plane'=32] {'layer'}, use_global_device_ids=true, to_apply=%region_8.10 | all-reduce | flops 4608 | bytes 36864 | tf_op jit(solution)/shard_map/psum | solution.py:207
  308.9 4.2 %collective-permute-start.5 = (f32[128]{0:T(128)S(1)}, f32[128]{0:T(128)S(1)}, u32[]{:S(2)}, u32[]{:S(2)}) collective-permute-start(f32[128]{0:T(128)S(1)} %get-tuple-element.525), channel_id=1, source_target_pairs={{0,2},{1,3},{2,4},{3,5},{4,6},{5,7},{6,8},{7,9},{8,10},{9,11},{10,... | collective-permute-start | bytes 1544 | tf_op jit(solution)/shard_map/ppermute | solution.py:16
  313.1 1.9 collective-permute-start.6
  315.0 5.5 %collective-permute-start.7 = (f32[128]{0:T(128)S(1)}, f32[128]{0:T(128)S(1)}, u32[]{:S(2)}, u32[]{:S(2)}) collective-permute-start(f32[128]{0:T(128)S(1)} %get-tuple-element.523), channel_id=1, source_target_pairs={{1,0},{2,1},{3,2},{4,3},{5,4},{6,5},{7,6},{8,7},{9,8},{10,9},{11,1... | collective-permute-start | bytes 1544 | tf_op jit(solution)/shard_map/ppermute | solution.py:16
  320.5 2.0 collective-permute-start.8
  322.5 1.3 scatter_fusion
  323.8 1.3 scatter_fusion.1
  325.1 1.3 scatter_fusion.2
  326.4 1.3 scatter_fusion.3
  (160 shorter events, 11.1 us)
Async XLA Ops:
  6.5 33.3 %copy-start.5 = (bf16[2,8,4096]{2,1,0:T(8,128)(2,1)S(1)}, bf16[2,8,4096]{2,1,0:T(8,128)(2,1)}, u32[]{:S(2)}) copy-start(bf16[2,8,4096]{2,1,0:T(8,128)(2,1)} %param.19) | copy-start | bytes 393220
  6.5 33.4 %copy-start.3 = (f32[8,4096]{1,0:T(8,128)S(1)}, f32[8,4096]{1,0:T(8,128)}, u32[]{:S(2)}) copy-start(f32[8,4096]{1,0:T(8,128)} %param.27) | copy-start | bytes 393220
  6.5 34.1 %copy-start.4 = (f32[8,4096]{1,0:T(8,128)S(1)}, f32[8,4096]{1,0:T(8,128)}, u32[]{:S(2)}) copy-start(f32[8,4096]{1,0:T(8,128)} %param.28) | copy-start | bytes 393220
  6.5 35.7 %copy-start.6 = (bf16[2,8,4096]{2,1,0:T(8,128)(2,1)S(1)}, bf16[2,8,4096]{2,1,0:T(8,128)(2,1)}, u32[]{:S(2)}) copy-start(bf16[2,8,4096]{2,1,0:T(8,128)(2,1)} %param.20) | copy-start | bytes 393220
  13.3 71.1 %copy-start.12 = (s32[4,128]{1,0:T(4,128)S(1)}, s32[4,128]{1,0:T(4,128)}, u32[]{:S(2)}) copy-start(s32[4,128]{1,0:T(4,128)} %param.22) | copy-start | bytes 6148
  16.5 68.5 %collective-permute-start = (bf16[4,8,128]{1,0,2:T(4,128)(2,1)S(1)}, bf16[4,8,128]{1,0,2:T(4,128)(2,1)S(1)}, u32[]{:S(2)}, u32[]{:S(2)}) collective-permute-start(bf16[4,8,128]{1,0,2:T(4,128)(2,1)S(1)} %select_bitcast_fusion.3), channel_id=1, source_target_pairs={{0,2},{1,3},{2,4},{3,5},{4,6},{5,7},{6,8},{7,9},{8,10},{9,11},{10,... | collective-permute-start | bytes 24584 | tf_op jit(solution)/shard_map/ppermute | solution.py:16
  23.9 61.2 %collective-permute-start.1 = (bf16[4,8,128]{1,0,2:T(4,128)(2,1)S(1)}, bf16[4,8,128]{1,0,2:T(4,128)(2,1)S(1)}, u32[]{:S(2)}, u32[]{:S(2)}) collective-permute-start(bf16[4,8,128]{1,0,2:T(4,128)(2,1)S(1)} %select_bitcast_fusion.2), channel_id=1, source_target_pairs={{0,1},{1,2},{2,3},{3,4},{4,5},{5,6},{6,7},{7,8},{8,9},{9,10},{10,1... | collective-permute-start | bytes 24584 | tf_op jit(solution)/shard_map/ppermute | solution.py:16
  30.3 54.9 %collective-permute-start.2 = (bf16[4,8,128]{1,0,2:T(4,128)(2,1)S(1)}, bf16[4,8,128]{1,0,2:T(4,128)(2,1)S(1)}, u32[]{:S(2)}, u32[]{:S(2)}) collective-permute-start(bf16[4,8,128]{1,0,2:T(4,128)(2,1)S(1)} %select_bitcast_fusion.1), channel_id=1, source_target_pairs={{1,0},{2,1},{3,2},{4,3},{5,4},{6,5},{7,6},{8,7},{9,8},{10,9},{11,1... | collective-permute-start | bytes 24584 | tf_op jit(solution)/shard_map/ppermute | solution.py:16
  37.6 54.8 %copy-start = (f32[8,4096]{1,0:T(8,128)S(1)}, f32[8,4096]{1,0:T(8,128)}, u32[]{:S(2)}) copy-start(f32[8,4096]{1,0:T(8,128)} %param.25) | copy-start | bytes 393220
  37.6 54.8 %copy-start.7 = (s32[4,4096]{1,0:T(4,128)S(1)}, s32[4,4096]{1,0:T(4,128)}, u32[]{:S(2)}) copy-start(s32[4,4096]{1,0:T(4,128)} %param.21) | copy-start | bytes 196612
  37.7 54.8 %copy-start.8 = (f32[24,8,1,1]{0,1,3,2:T(8,128)S(1)}, f32[24,8,1,1]{0,1,3,2:T(8,128)}, u32[]{:S(2)}) copy-start(f32[24,8,1,1]{0,1,3,2:T(8,128)} %constant.375) | copy-start | bytes 2308
  37.7 47.6 %collective-permute-start.3 = (bf16[4,8,128]{1,0,2:T(4,128)(2,1)S(1)}, bf16[4,8,128]{1,0,2:T(4,128)(2,1)S(1)}, u32[]{:S(2)}, u32[]{:S(2)}) collective-permute-start(bf16[4,8,128]{1,0,2:T(4,128)(2,1)S(1)} %select_bitcast_fusion), channel_id=1, source_target_pairs={{2,0},{3,1},{4,2},{5,3},{6,4},{7,5},{8,6},{9,7},{10,8},{11,9},{12,... | collective-permute-start | bytes 24584 | tf_op jit(solution)/shard_map/ppermute | solution.py:16
  84.4 6.5 %copy-start.1 = (f32[4096]{0:T(1024)}, f32[4096]{0:T(1024)S(1)}, u32[]{:S(2)}) copy-start(f32[4096]{0:T(1024)S(1)} %get-tuple-element.341) | copy-start | bytes 49156
  85.5 5.3 %collective-permute-start.4 = (bf16[4,4608]{1,0:T(4,128)(2,1)S(1)}, bf16[4,4608]{1,0:T(4,128)(2,1)S(1)}, u32[]{:S(2)}, u32[]{:S(2)}) collective-permute-start(bf16[4,4608]{1,0:T(4,128)(2,1)S(1)} %bitcast.276), channel_id=1, source_target_pairs={{32,0},{64,32},{96,64},{128,96},{160,128},{192,160},{224,192},{256... | collective-permute-start | bytes 110600 | tf_op jit(solution)/shard_map/ppermute | solution.py:16
  92.5 163.3 %copy-start.2 = (f32[4096]{0:T(1024)S(1)}, f32[4096]{0:T(1024)}, u32[]{:S(2)}) copy-start(f32[4096]{0:T(1024)} %copy-done.1) | copy-start | bytes 49156
  92.5 163.3 %copy-start.9 = (f32[1,4096]{1,0:T(1,128)S(1)}, f32[1,4096]{1,0:T(1,128)}, u32[]{:S(2)}) copy-start(f32[1,4096]{1,0:T(1,128)} %get-tuple-element.501) | copy-start | bytes 49156
  92.5 163.3 %copy-start.10 = (f32[1,4096]{1,0:T(1,128)S(1)}, f32[1,4096]{1,0:T(1,128)}, u32[]{:S(2)}) copy-start(f32[1,4096]{1,0:T(1,128)} %get-tuple-element.502) | copy-start | bytes 49156
  92.5 163.3 %copy-start.11 = (f32[1,4096]{1,0:T(1,128)S(1)}, f32[1,4096]{1,0:T(1,128)}, u32[]{:S(2)}) copy-start(f32[1,4096]{1,0:T(1,128)} %get-tuple-element.503) | copy-start | bytes 49156
  255.6 66.9 %copy-start.16 = (s32[128]{0:T(128)S(1)}, s32[128]{0:T(128)}, u32[]{:S(2)}) copy-start(s32[128]{0:T(128)} %get-tuple-element.529) | copy-start | bytes 1540
  256.7 67.1 %copy-start.15 = (s32[128]{0:T(128)S(1)}, s32[128]{0:T(128)}, u32[]{:S(2)}) copy-start(s32[128]{0:T(128)} %get-tuple-element.528) | copy-start | bytes 1540
  256.7 68.4 %copy-start.14 = (s32[128]{0:T(128)S(1)}, s32[128]{0:T(128)}, u32[]{:S(2)}) copy-start(s32[128]{0:T(128)} %get-tuple-element.527) | copy-start | bytes 1540
  256.7 69.7 %copy-start.13 = (s32[128]{0:T(128)S(1)}, s32[128]{0:T(128)}, u32[]{:S(2)}) copy-start(s32[128]{0:T(128)} %get-tuple-element.526) | copy-start | bytes 1540
  308.9 13.6 %collective-permute-start.5 = (f32[128]{0:T(128)S(1)}, f32[128]{0:T(128)S(1)}, u32[]{:S(2)}, u32[]{:S(2)}) collective-permute-start(f32[128]{0:T(128)S(1)} %get-tuple-element.525), channel_id=1, source_target_pairs={{0,2},{1,3},{2,4},{3,5},{4,6},{5,7},{6,8},{7,9},{8,10},{9,11},{10,... | collective-permute-start | bytes 1544 | tf_op jit(solution)/shard_map/ppermute | solution.py:16
  313.1 10.7 %collective-permute-start.6 = (f32[128]{0:T(128)S(1)}, f32[128]{0:T(128)S(1)}, u32[]{:S(2)}, u32[]{:S(2)}) collective-permute-start(f32[128]{0:T(128)S(1)} %get-tuple-element.524), channel_id=1, source_target_pairs={{0,1},{1,2},{2,3},{3,4},{4,5},{5,6},{6,7},{7,8},{8,9},{9,10},{10,1... | collective-permute-start | bytes 1544 | tf_op jit(solution)/shard_map/ppermute | solution.py:16
  315.0 10.1 %collective-permute-start.7 = (f32[128]{0:T(128)S(1)}, f32[128]{0:T(128)S(1)}, u32[]{:S(2)}, u32[]{:S(2)}) collective-permute-start(f32[128]{0:T(128)S(1)} %get-tuple-element.523), channel_id=1, source_target_pairs={{1,0},{2,1},{3,2},{4,3},{5,4},{6,5},{7,6},{8,7},{9,8},{10,9},{11,1... | collective-permute-start | bytes 1544 | tf_op jit(solution)/shard_map/ppermute | solution.py:16
  320.5 5.9 %collective-permute-start.8 = (f32[128]{0:T(128)S(1)}, f32[128]{0:T(128)S(1)}, u32[]{:S(2)}, u32[]{:S(2)}) collective-permute-start(f32[128]{0:T(128)S(1)} %get-tuple-element.522), channel_id=1, source_target_pairs={{2,0},{3,1},{4,2},{5,3},{6,4},{7,5},{8,6},{9,7},{10,8},{11,9},{12,... | collective-permute-start | bytes 1544 | tf_op jit(solution)/shard_map/ppermute | solution.py:16
where the time goes:
time: 335 us; the launch traced here: 328 us
  matrix products  86.7 us (26%)
  blocking collectives  83.2 us (25%)
  other arithmetic  82.7 us (25%)
  local copies, waits for them, and re-layouts  33.9 us (10%)
  starting transfers between devices  29.5 us (9%)
  loops' own time  8.69 us (3%)
    dot_general x4, matrix products, one_block(): jnp.dot(level_table, high_select(corner_ids, high_count, jnp.bfloat16), p...  63.9 us
    reduce_sum x4, other arithmetic, one_block(): nodal_values = jnp.sum(picked * low_select(corner_ids)[None], axis=1)  59.2 us
    psum x1, blocking collectives, shards(): summed = lax.psum(partial_nodes, 'layer')  42.5 us
    all_gather x2, blocking collectives, entering_2(): everything = jax.tree.map(lambda part: lax.all_gather(part, axis), value)  40.7 us
    ppermute x9, starting transfers between devices, shifted(): lax.ppermute(value, axis, [(source, source + steps) for source in range(f...  29.5 us
    dot_general x4, matrix products, element_terms(): jnp.einsum('rn,clnb->clrb', basis, hexa_nodes, precision=lax.Precision.HI...  14.5 us
    gather x4, local copies, waits for them, and re-layouts, shards(): jnp.take(padded, shared[direction], axis=2)  11.8 us
    dot_general x4, matrix products, add_block(): jnp.dot(low_values, high_select(corner_ids, high_count, jnp.float32).T, p...  8.37 us
  transfers between devices with their start and end apart: 9, of which 1 were waited for; matrix products, arithmetic and copies ran while one was open for 5% of the time, Pallas kernels for 0%

commit v1 on v0

v1 whole, which is shorter than its diff:
```python
import functools
import math

import jax
import jax.numpy as jnp
from jax import lax
from jax.experimental import pallas as pl
from jax.experimental.pallas import tpu as pltpu
from jax.sharding import PartitionSpec as P

OFFSETS = (-2, -1, 1, 2)
STRAIN_EPS = 0.01
GAUSS = 1.0 / math.sqrt(3.0)
MESH = pl.DeviceIdType.MESH
WIDE = 256
OWN_ROWS = 16
ALL_ROWS = 18
MAIN_BLOCK = 512
SCATTER_BLOCK = 1024


def iota(shape, axis):
    return lax.broadcasted_iota(jnp.int32, shape, axis)


def one_hot(low, width):
    return (iota((width, low.shape[1]), 0) == low).astype(jnp.float32).astype(jnp.bfloat16)


def pick(row, size, table, count):
    out = table[0:size]
    for i in range(1, count):
        out = jnp.where(row == i, table[i * size : (i + 1) * size], out)
    return out


def corner_modes(v):
    p, q, r, s = v[1] - v[0], v[2] - v[3], v[0] + v[1], v[2] + v[3]
    return r + s, p + q, s - r, q - p


def element_terms(upper, lowest, stretch, shear, thick, rate):
    n = thick.shape[1]
    last = iota((8, n), 0) == 7
    top, end = corner_modes(upper), corner_modes(lowest)
    derived = []
    for comp in range(4):
        half, diff = [], []
        for m in range(4):
            t = top[m][comp * 8 : (comp + 1) * 8]
            b = jnp.where(last, pltpu.roll(end[m], 7 - comp, 0), pltpu.roll(t, 7, 0))
            d = t - b
            diff.append(d)
            if m:
                mean = t + b
                gd = GAUSS * d
                half.append((mean - gd, mean + gd))
        mx, my, mxy = half
        xi, eta = [], []
        for z in range(2):
            t = GAUSS * mxy[z]
            xi.append((mx[z] - t, mx[z] + t))
            eta.append((my[z] - t, my[z] + t))
        d0, dx, dy, dxy = diff
        gx, gy, gxy = GAUSS * dx, GAUSS * dy, (GAUSS * GAUSS) * dxy
        a0, a1, b0, b1 = d0 - gx, d0 + gx, gy - gxy, gy + gxy
        derived.append((xi, eta, ((a0 - b0, a0 + b0), (a1 - b1, a1 + b1))))
    s0, s1 = 0.125 * stretch[0:1], 0.125 * stretch[1:2]
    h0, h1 = 0.125 * shear[0:1], 0.125 * shear[1:2]
    inv = 0.125 / thick

    def strains(first, second):
        axi, aeta, az = derived[first]
        bxi, beta, bz = derived[second]
        two = range(2)
        return (
            [[s0 * axi[z][e] for e in two] for z in two],
            [[h0 * aeta[z][x] for x in two] for z in two],
            [[h1 * bxi[z][e] for e in two] for z in two],
            [[s1 * beta[z][x] for x in two] for z in two],
            [[h1 * axi[z][e] + s0 * bxi[z][e] for e in two] for z in two],
            [[s1 * aeta[z][x] + h0 * beta[z][x] for x in two] for z in two],
            [[inv * az[x][e] for e in two] for x in two],
            [[inv * bz[x][e] for e in two] for x in two],
        )

    f, g = strains(0, 1), strains(2, 3)
    total = None
    for x in range(2):
        for e in range(2):
            fxz, fyz, gxz, gyz = f[6][x][e], f[7][x][e], g[6][x][e], g[7][x][e]
            own_z = fxz * fxz + fyz * fyz + STRAIN_EPS
            cross_z = fxz * gxz + fyz * gyz
            for z in range(2):
                fxx, fyy = f[0][z][e] + f[1][z][x], f[2][z][e] + f[3][z][x]
                fxy = 0.5 * (f[4][z][e] + f[5][z][x])
                gxx, gyy = g[0][z][e] + g[1][z][x], g[2][z][e] + g[3][z][x]
                gxy = 0.5 * (g[4][z][e] + g[5][z][x])
                a, b = fxx + 0.5 * fyy, fyy + 0.5 * fxx
                effective = fxx * a + fyy * b + fxy * fxy + own_z
                cross = gxx * a + gyy * b + fxy * gxy + cross_z
                term = jnp.exp2((-1.0 / 3.0) * jnp.log2(effective)) * cross
                total = term if total is None else total + term
    det = stretch[0:1] * stretch[1:2] - shear[0:1] * shear[1:2]
    return (rate * thick) * (total / det)


def recurrence(keep, wei):
    sub = iota(keep.shape, 0)
    factor, offset = keep, (1.0 - keep) * wei
    for d in (1, 2, 4):
        before_f = jnp.where(sub >= d, pltpu.roll(factor, d, 0), 1.0)
        before_o = jnp.where(sub >= d, pltpu.roll(offset, d, 0), 0.0)
        offset = factor * before_o + offset
        factor = factor * before_f
    return factor, offset


def split_bf16(x):
    high = x.astype(jnp.bfloat16).astype(jnp.float32)
    return high, x - high


def kernel(
    layers,
    planes,
    vel_hbm, adj_hbm, cor_hbm, sha_hbm, str_hbm, she_hbm, thi_hbm, rat_hbm, ret_hbm, wei_hbm,
    out,
    vel, adj, corners, shared, stretch, shear, thick, rate, ret, wei,
    table, table8, low_send, low_own, gsend, grecv, lsend, lrecv,
    fac, off, sc_send, sc_recv, en_send, en_recv,
    abuf, bbuf, acc,
    rs_send, rs_recv, gh_send, gh_recv, ag_send, ag_recv,
    in_sem, low_s, low_r, g_s, g_r, l_s, l_r, sc_s, sc_r, en_s, en_r, rs_s, rs_r, gh_s, gh_r, ag_s, ag_r,
):
    g, p = lax.axis_index("layer"), lax.axis_index("plane")
    per = OWN_ROWS // layers
    f32, bf16 = jnp.float32, jnp.bfloat16

    hbm = (vel_hbm, adj_hbm, sha_hbm, ret_hbm, wei_hbm, cor_hbm, str_hbm, she_hbm, thi_hbm, rat_hbm)
    own = (vel, adj, shared, ret, wei, corners, stretch, shear, thick, rate)
    loads = [pltpu.make_async_copy(a, b, in_sem.at[i]) for i, (a, b) in enumerate(zip(hbm, own))]
    for load in loads:
        load.start()

    valid = [jnp.logical_and(p + o >= 0, p + o < planes) for o in OFFSETS]
    up, down = g > 0, g < layers - 1

    for d in range(4):
        @pl.when(jnp.logical_not(valid[d]))
        def _():
            grecv[d] = jnp.zeros(grecv.shape[1:], bf16)
            lrecv[d] = jnp.zeros(lrecv.shape[1:], bf16)
            gh_recv[d] = jnp.zeros(gh_recv.shape[1:], f32)

    @pl.when(jnp.logical_not(down))
    def _():
        low_own[...] = jnp.zeros(low_own.shape, bf16)
        lrecv[...] = jnp.zeros(lrecv.shape, bf16)

    barrier = pltpu.get_barrier_semaphore()

    def greet(layer, plane):
        pl.semaphore_signal(barrier, inc=1, device_id=(layer, plane), device_id_type=MESH)

    def greet_layer(r, _):
        greet(lax.rem(g + r, layers), p)
        return 0

    lax.fori_loop(1, layers, greet_layer, 0)
    expected = layers - 1
    for d, o in enumerate(OFFSETS):
        @pl.when(valid[d])
        def _():
            greet(g, p + o)

        @pl.when(jnp.logical_and(valid[d], up))
        def _():
            greet(g - 1, p + o)

        @pl.when(jnp.logical_and(valid[d], down))
        def _():
            greet(g + 1, p + o)

        expected = expected + valid[d].astype(jnp.int32) * (1 + up.astype(jnp.int32) + down.astype(jnp.int32))

    loads[0].wait()
    loads[1].wait()
    for i in range(OWN_ROWS):
        at = slice(i * WIDE, (i + 1) * WIDE)
        table[i * 32 : (i + 1) * 32] = jnp.concatenate(
            [vel[0, :, at], vel[1, :, at], adj[0, :, at], adj[1, :, at]], axis=0
        )
    row8 = iota((8, WIDE), 0)
    pieces = []
    for i in range(0, OWN_ROWS, 2):
        piece = jnp.zeros((8, WIDE), f32)
        for half in range(2):
            for comp in range(4):
                level = (vel, adj)[comp // 2][comp % 2, :, (i + half) * WIDE : (i + half + 1) * WIDE].astype(f32)
                piece = jnp.where(row8 == half * 4 + comp, level[0:1], piece)
        pieces.append(piece)
    low_send[...] = jnp.concatenate(pieces, axis=0).astype(bf16)
    loads[2].wait()
    row16 = iota((16, 128), 0)
    for j in range(4):
        ids = shared[j : j + 1, :]
        sent = jnp.dot(table[0 : OWN_ROWS * 32], one_hot(ids & (WIDE - 1), WIDE), preferred_element_type=f32)
        sent = pick(ids >> 8, 32, sent, OWN_ROWS)
        gsend[j] = sent.astype(bf16)
        tops = jnp.zeros((16, 128), f32)
        for comp in range(4):
            tops = jnp.where(row16 == comp, sent[comp * 8 : comp * 8 + 1], tops)
        lsend[j] = tops.astype(bf16)
    loads[3].wait()
    loads[4].wait()
    for i in range(8):
        at = slice(i * 512, (i + 1) * 512)
        factor, offset = recurrence(ret[:, at], wei[:, at])
        fac[:, at] = factor
        off[:, at] = offset
    for i in range(layers):
        for k in range(per):
            at = slice((i * per + k) * WIDE, (i * per + k + 1) * WIDE)
            sc_send[i, k : k + 1, :] = fac[7:8, at]
            sc_send[i, per + k : per + k + 1, :] = off[7:8, at]

    pl.semaphore_wait(barrier, expected)

    def remote(src, dst, s, r, layer, plane):
        return pltpu.make_async_remote_copy(
            src_ref=src, dst_ref=dst, send_sem=s, recv_sem=r, device_id=(layer, plane), device_id_type=MESH
        )

    def to_all(send, recv, s, r, same=False):
        def copy(i):
            return remote(send if same else send.at[i], recv.at[g], s.at[i], r.at[g], i, p)

        def start(k, _):
            copy(lax.rem(g + k, layers)).start()
            return 0

        lax.fori_loop(1, layers, start, 0)

    def from_all(send, recv, s, r, same=False):
        def wait(k, _):
            i = lax.rem(g + k, layers)
            remote(send if same else send.at[i], recv.at[i], s.at[i], r.at[i], i, p).wait_recv()
            return 0

        lax.fori_loop(1, layers, wait, 0)

    def sent_all(send, recv, s, r, same=False):
        def wait(k, _):
            i = lax.rem(g + k, layers)
            remote(send if same else send.at[i], recv.at[i], s.at[i], r.at[i], i, p).wait_send()
            return 0

        lax.fori_loop(1, layers, wait, 0)

    def ghost(j):
        return remote(gsend.at[j], grecv.at[3 - j], g_s.at[j], g_r.at[3 - j], g, p + OFFSETS[j])

    def low_ghost(j):
        return remote(lsend.at[j], lrecv.at[3 - j], l_s.at[j], l_r.at[3 - j], g - 1, p + OFFSETS[j])

    low_copy = remote(low_send, low_own, low_s, low_r, g - 1, p)

    to_all(sc_send, sc_recv, sc_s, sc_r)
    for j in range(4):
        @pl.when(valid[j])
        def _():
            ghost(j).start()

        @pl.when(jnp.logical_and(valid[j], up))
        def _():
            low_ghost(j).start()

    @pl.when(up)
    def _():
        low_copy.start()

    sc_recv[g] = sc_send[g]
    from_all(sc_send, sc_recv, sc_s, sc_r)
    running = jnp.zeros((per, WIDE), f32)
    for i in range(layers):
        en_send[i] = running
        running = sc_recv[i, 0:per, :] * running + sc_recv[i, per : 2 * per, :]
    to_all(en_send, en_recv, en_s, en_r)
    en_recv[g] = en_send[g]

    for load in loads[5:]:
        load.wait()

    for j in range(4):
        @pl.when(valid[j])
        def _():
            remote(gsend.at[j], grecv.at[j], g_s.at[j], g_r.at[j], g, p + OFFSETS[j]).wait_recv()

        @pl.when(jnp.logical_and(valid[j], down))
        def _():
            remote(lsend.at[j], lrecv.at[j], l_s.at[j], l_r.at[j], g, p + OFFSETS[j]).wait_recv()

    @pl.when(down)
    def _():
        low_copy.wait_recv()

    for i in range(2):
        table[(OWN_ROWS + i) * 32 : (OWN_ROWS + i + 1) * 32] = jnp.concatenate([grecv[2 * i], grecv[2 * i + 1]], axis=1)
    table8[0:64] = low_own[...]
    first = jnp.concatenate([lrecv[0], lrecv[1]], axis=1).astype(f32)[0:8]
    second = jnp.concatenate([lrecv[2], lrecv[3]], axis=1).astype(f32)[0:8]
    ghosts8 = first + pltpu.roll(second, 4, 0)
    table8[64:80] = jnp.concatenate([ghosts8, jnp.zeros((8, WIDE), f32)], axis=0).astype(bf16)

    def main_block(b, _):
        at = pl.ds(pl.multiple_of(b * MAIN_BLOCK, MAIN_BLOCK), MAIN_BLOCK)
        upper, lowest = [], []
        for c in range(4):
            ids = corners[c : c + 1, at]
            row = ids >> 8
            hot = one_hot(ids & (WIDE - 1), WIDE)
            upper.append(pick(row, 32, jnp.dot(table[...], hot, preferred_element_type=f32), ALL_ROWS))
            both = pick(row >> 1, 8, jnp.dot(table8[...], hot, preferred_element_type=f32), ALL_ROWS // 2)
            lowest.append(jnp.where((row & 1) == 1, pltpu.roll(both, 4, 0), both))
        term = element_terms(upper, lowest, stretch[:, at], shear[:, at], thick[:, at], rate[:, at])
        abuf[:, at] = jnp.sum(fac[:, at] * term, axis=0, keepdims=True)
        bbuf[:, at] = jnp.sum(off[:, at] * term, axis=0, keepdims=True)
        return 0

    lax.fori_loop(0, corners.shape[1] // MAIN_BLOCK, main_block, 0)

    from_all(en_send, en_recv, en_s, en_r)
    for i in range(layers):
        for k in range(per):
            at = slice((i * per + k) * WIDE, (i * per + k + 1) * WIDE)
            abuf[:, at] = 0.25 * (abuf[:, at] * en_recv[i, k : k + 1, :] + bbuf[:, at])

    acc[...] = jnp.zeros(acc.shape, f32)

    def scatter_block(b, _):
        at = pl.ds(pl.multiple_of(b * SCATTER_BLOCK, SCATTER_BLOCK), SCATTER_BLOCK)
        row48 = iota((48, SCATTER_BLOCK), 0)
        high, low = split_bf16(abuf[:, at])
        value = jnp.where(row48 < 24, high, low)
        place = jnp.where(row48 < 24, row48, row48 - 24)
        out48 = None
        for c in range(4):
            ids = corners[c : c + 1, at]
            spread = jnp.where(place == (ids >> 8), value, 0.0).astype(bf16)
            part = lax.dot_general(
                one_hot(ids & (WIDE - 1), WIDE), spread, (((1,), (1,)), ((), ())), preferred_element_type=f32
            )
            out48 = part if out48 is None else out48 + part
        acc[...] += out48
        return 0

    lax.fori_loop(0, corners.shape[1] // SCATTER_BLOCK, scatter_block, 0)
    nodes = acc[...].T
    nodes = nodes[0:24] + nodes[24:48]
    for i in range(layers):
        for k in range(per):
            lo = i * per + k
            rs_send[i, 2 * k : 2 * k + 1, :] = nodes[lo : lo + 1, 0:128]
            rs_send[i, 2 * k + 1 : 2 * k + 2, :] = nodes[lo : lo + 1, 128:256]
    for j in range(4):
        gh_send[j] = nodes[OWN_ROWS + j // 2 : OWN_ROWS + j // 2 + 1, (j % 2) * 128 : (j % 2 + 1) * 128]

    def ghost_sum(j):
        return remote(gh_send.at[j], gh_recv.at[3 - j], gh_s.at[j], gh_r.at[3 - j], g, p + OFFSETS[j])

    for j in range(4):
        @pl.when(valid[j])
        def _():
            ghost_sum(j).start()
    to_all(rs_send, rs_recv, rs_s, rs_r)
    rs_recv[g] = rs_send[g]

    hots, spots = [], []
    row64 = iota((64, 128), 0) & 31
    for d in range(4):
        ids = shared[d : d + 1, :]
        hots.append(one_hot(ids & 127, 128))
        spots.append(row64 == (ids >> 7))

    for j in range(4):
        @pl.when(valid[j])
        def _():
            remote(gh_send.at[j], gh_recv.at[j], gh_s.at[j], gh_r.at[j], g, p + OFFSETS[j]).wait_recv()
    from_all(rs_send, rs_recv, rs_s, rs_r)
    total = rs_recv[0]
    for i in range(1, layers):
        total = total + rs_recv[i]
    ag_send[0 : 2 * per] = total
    for d in range(4):
        ag_send[2 * per + d : 2 * per + d + 1] = gh_recv[d]
    spare = ag_send.shape[0] - 2 * per - 4
    if spare:
        ag_send[2 * per + 4 :] = jnp.zeros((spare, 128), f32)
    to_all(ag_send, ag_recv, ag_s, ag_r, same=True)
    ag_recv[g] = ag_send[...]
    from_all(ag_send, ag_recv, ag_s, ag_r, same=True)

    arrived = ag_recv[0]
    for i in range(1, layers):
        arrived = arrived + ag_recv[i]
    result = jnp.concatenate([ag_recv[i, 0 : 2 * per, :] for i in range(layers)], axis=0)
    added = None
    half64 = iota((64, 128), 0) < 32
    for d in range(4):
        high, low = split_bf16(arrived[2 * per + d : 2 * per + d + 1])
        spread = jnp.where(spots[d], jnp.where(half64, high, low), 0.0).astype(bf16)
        part = lax.dot_general(spread, hots[d], (((1,), (1,)), ((), ())), preferred_element_type=f32)
        added = part if added is None else added + part
    out[...] = result + (added[0:32] + added[32:64])

    sent_all(sc_send, sc_recv, sc_s, sc_r)
    sent_all(en_send, en_recv, en_s, en_r)
    sent_all(rs_send, rs_recv, rs_s, rs_r)
    sent_all(ag_send, ag_recv, ag_s, ag_r, same=True)
    for j in range(4):
        @pl.when(valid[j])
        def _():
            ghost(j).wait_send()
            ghost_sum(j).wait_send()

        @pl.when(jnp.logical_and(valid[j], up))
        def _():
            low_ghost(j).wait_send()

    @pl.when(up)
    def _():
        low_copy.wait_send()


def shards(layers, planes, *args):
    velocity, adjoint, corners, shared, stretch, shear_part, thickness, rate_factor, retention, weight = args
    per = OWN_ROWS // layers
    elems = corners.shape[1]
    gathered = -(-(2 * per + 4) // 8) * 8
    f32, bf16 = jnp.float32, jnp.bfloat16
    vmem, dma = pltpu.VMEM, pltpu.SemaphoreType.DMA
    out = pl.pallas_call(
        functools.partial(kernel, layers, planes),
        out_shape=jax.ShapeDtypeStruct((32, 128), f32),
        in_specs=[pl.BlockSpec(memory_space=pl.ANY)] * 10,
        out_specs=pl.BlockSpec(memory_space=pltpu.VMEM),
        scratch_shapes=[vmem(a.shape, a.dtype) for a in args]
        + [
            vmem((ALL_ROWS * 32, WIDE), bf16), vmem((80, WIDE), bf16),
            vmem((64, WIDE), bf16), vmem((64, WIDE), bf16),
            vmem((4, 32, 128), bf16), vmem((4, 32, 128), bf16),
            vmem((4, 16, 128), bf16), vmem((4, 16, 128), bf16),
            vmem((8, elems), f32), vmem((8, elems), f32),
            vmem((layers, 2 * per, WIDE), f32), vmem((layers, 2 * per, WIDE), f32),
            vmem((layers, per, WIDE), f32), vmem((layers, per, WIDE), f32),
            vmem((1, elems), f32), vmem((1, elems), f32), vmem((WIDE, 48), f32),
            vmem((layers, 2 * per, 128), f32), vmem((layers, 2 * per, 128), f32),
            vmem((4, 1, 128), f32), vmem((4, 1, 128), f32),
            vmem((gathered, 128), f32), vmem((layers, gathered, 128), f32),
            dma((10,)), dma, dma, dma((4,)), dma((4,)), dma((4,)), dma((4,)),
        ]
        + [dma((layers,)), dma((layers,)), dma((layers,)), dma((layers,)), dma((layers,)), dma((layers,)), dma((4,)), dma((4,)), dma((layers,)), dma((layers,))],
        compiler_params=pltpu.CompilerParams(collective_id=0, has_side_effects=True, vmem_limit_bytes=40 << 20),
        name="ice_gradient",
    )(*args)
    return out.reshape(4096)


def solution(mesh):
    return jax.shard_map(
        functools.partial(shards, mesh.shape["layer"], mesh.shape["plane"]),
        mesh=mesh,
        in_specs=(
            P(None, "layer", "plane"),
            P(None, "layer", "plane"),
            P(None, "plane"),
            P(None, "plane"),
            P(None, "plane"),
            P(None, "plane"),
            P("layer", "plane"),
            P("layer", "plane"),
            P("layer", "plane"),
            P("layer", "plane"),
        ),
        out_specs=P("plane"),
        check_vma=False,
    )
```

time: 335 us -> 55.6 us (0.17); the launches traced: 328 us -> 55.2 us
  matrix products: 86.7 us -> 0 us
  blocking collectives: 83.2 us -> 0 us
  other arithmetic: 82.7 us -> 0 us
  Pallas kernels: 0 us -> 46.1 us
  starting transfers between devices: 29.5 us -> 0 us
  local copies, waits for them, and re-layouts: 33.9 us -> 9.06 us
  loops' own time: 8.69 us -> 0 us
    dot_general x12 -> x0, matrix products: 86.7 us -> none  [the longest x4 63.9 us: one_block(): jnp.dot(level_table, high_select(corner_ids, high_count, jnp.bfloat16), p...]
    reduce_sum x8 -> x0, other arithmetic: 62 us -> none  [the longest x4 59.2 us: one_block(): nodal_values = jnp.sum(picked * low_select(corner_ids)[None], axis=1)]
    pallas_call x0 -> x1, Pallas kernels: none -> 46.1 us  [shards(): pl.pallas_call(functools.partial(kernel, layers, planes), out_shape=jax.S...]
    psum x1 -> x0, blocking collectives: 42.5 us -> none  [shards(): summed = lax.psum(partial_nodes, 'layer')]
    all_gather x2 -> x0, blocking collectives: 40.7 us -> none  [entering_2(): everything = jax.tree.map(lambda part: lax.all_gather(part, axis), value)]
    ppermute x9 -> x0, starting transfers between devices: 29.5 us -> none  [shifted(): lax.ppermute(value, axis, [(source, source + steps) for source in range(f...]
    gather x4 -> x0, local copies, waits for them, and re-layouts: 11.8 us -> none  [shards(): jnp.take(padded, shared[direction], axis=2)]
    concatenate x3 -> x0, local copies, waits for them, and re-layouts: 11.4 us -> none  [the longest x1 6.84 us: shards(): jnp.concatenate([fields, jnp.zeros((4, layer_count, 1), fields.dtype)], a...]
  transfers between devices with their start and end apart: 9 -> 0, of which waited for: 1 -> 0; matrix products, arithmetic and copies ran while one was open for 5% -> 0% of each run, Pallas kernels for 0% -> 0%
where the time goes in v1:
time: 55.6 us; the launch traced here: 55.2 us
  Pallas kernels  46.1 us (83%)
  local copies, waits for them, and re-layouts  9.06 us (16%)
    pallas_call x1, Pallas kernels, shards(): pl.pallas_call(functools.partial(kernel, layers, planes), out_shape=jax.S...  46.1 us
    unnamed x21, local copies, waits for them, and re-layouts  9.06 us

profile of v1, /device:TPU:7, one launch (start us, length us, event | category | flops | bytes accessed | tf_op | source)
XLA Modules:
  0.0 55.2 jit_solution(12091962250601047941)
XLA Ops:
  0.0 0.0 copy-start
  0.0 0.9 %copy-done = bf16[2,8,4096]{2,1,0:T(8,128)(2,1)S(1)} copy-done((bf16[2,8,4096]{2,1,0:T(8,128)(2,1)S(1)}, bf16[2,8,4096]{2,1,0:T(8,128)(2,1)}, u32[]{:S(2)}) %copy-start) | copy-done | bytes 131096
  0.9 0.0 copy-start.1
  0.9 0.9 %copy-done.1 = bf16[2,8,4096]{2,1,0:T(8,128)(2,1)S(1)} copy-done((bf16[2,8,4096]{2,1,0:T(8,128)(2,1)S(1)}, bf16[2,8,4096]{2,1,0:T(8,128)(2,1)}, u32[]{:S(2)}) %copy-start.1) | copy-done | bytes 131096
  1.8 0.0 copy-start.2
  1.8 0.9 %copy-done.2 = f32[8,4096]{1,0:T(8,128)S(1)} copy-done((f32[8,4096]{1,0:T(8,128)S(1)}, f32[8,4096]{1,0:T(8,128)}, u32[]{:S(2)}) %copy-start.2) | copy-done | bytes 131096
  2.7 0.0 copy-start.3
  2.7 0.9 %copy-done.3 = f32[8,4096]{1,0:T(8,128)S(1)} copy-done((f32[8,4096]{1,0:T(8,128)S(1)}, f32[8,4096]{1,0:T(8,128)}, u32[]{:S(2)}) %copy-start.3) | copy-done | bytes 131096
  3.6 0.0 copy-start.4
  3.6 0.9 %copy-done.4 = f32[8,4096]{1,0:T(8,128)S(1)} copy-done((f32[8,4096]{1,0:T(8,128)S(1)}, f32[8,4096]{1,0:T(8,128)}, u32[]{:S(2)}) %copy-start.4) | copy-done | bytes 131096
  4.5 0.0 copy-start.5
  4.5 0.9 %copy-done.5 = f32[8,4096]{1,0:T(8,128)S(1)} copy-done((f32[8,4096]{1,0:T(8,128)S(1)}, f32[8,4096]{1,0:T(8,128)}, u32[]{:S(2)}) %copy-start.5) | copy-done | bytes 131096
  5.4 0.0 copy-start.6
  5.4 0.8 %copy-done.6 = s32[4,4096]{1,0:T(4,128)S(1)} copy-done((s32[4,4096]{1,0:T(4,128)S(1)}, s32[4,4096]{1,0:T(4,128)}, u32[]{:S(2)}) %copy-start.6) | copy-done | bytes 65560
  6.3 0.0 copy-start.7
  6.3 0.8 %copy-done.7 = f32[2,4096]{1,0:T(2,128)S(1)} copy-done((f32[2,4096]{1,0:T(2,128)S(1)}, f32[2,4096]{1,0:T(2,128)}, u32[]{:S(2)}) %copy-start.7) | copy-done | bytes 32792
  7.0 0.0 copy-start.8
  7.0 0.8 %copy-done.8 = f32[2,4096]{1,0:T(2,128)S(1)} copy-done((f32[2,4096]{1,0:T(2,128)S(1)}, f32[2,4096]{1,0:T(2,128)}, u32[]{:S(2)}) %copy-start.8) | copy-done | bytes 32792
  7.8 0.0 copy-start.9
  7.8 0.7 %copy-done.9 = s32[4,128]{1,0:T(4,128)S(1)} copy-done((s32[4,128]{1,0:T(4,128)S(1)}, s32[4,128]{1,0:T(4,128)}, u32[]{:S(2)}) %copy-start.9) | copy-done | bytes 2072
  8.5 46.1 %ice_gradient.1 = f32[32,128]{1,0:T(8,128)S(1)} custom-call(bf16[2,8,4096]{2,1,0:T(8,128)(2,1)S(1)} %copy-done, bf16[2,8,4096]{2,1,0:T(8,128)(2,1)S(1)} %copy-done.1, s32[4,4096]{1,0:T(4,128)S(1)} %copy-done.6, s32[4,128]{1,0:T(4,128)S(1)} %copy-done.9, f32[2,4096]{1,0:T(2,128)S(1)} %copy-done.7, f32[2,4096]{1,0:T(2,128)S(1)} %copy-done.8, ...), custom_call_target="tpu_custom_call" | custom-call | tf_op jit(solution)/shard_map/ice_gradient/pallas_call | solution.py:443
  54.6 0.6 %copy.12 = f32[4096]{0:T(1024)} copy(f32[4096]{0:T(1024)S(1)} %bitcast.1) | data formatting | bytes 32768
Async XLA Ops:
  0.0 0.9 %copy-start = (bf16[2,8,4096]{2,1,0:T(8,128)(2,1)S(1)}, bf16[2,8,4096]{2,1,0:T(8,128)(2,1)}, u32[]{:S(2)}) copy-start(bf16[2,8,4096]{2,1,0:T(8,128)(2,1)} %vel_hbm.1) | copy-start | bytes 393220
  0.9 0.9 %copy-start.1 = (bf16[2,8,4096]{2,1,0:T(8,128)(2,1)S(1)}, bf16[2,8,4096]{2,1,0:T(8,128)(2,1)}, u32[]{:S(2)}) copy-start(bf16[2,8,4096]{2,1,0:T(8,128)(2,1)} %adj_hbm.1) | copy-start | bytes 393220
  1.8 0.9 %copy-start.2 = (f32[8,4096]{1,0:T(8,128)S(1)}, f32[8,4096]{1,0:T(8,128)}, u32[]{:S(2)}) copy-start(f32[8,4096]{1,0:T(8,128)} %thi_hbm.1) | copy-start | bytes 393220
  2.7 0.9 %copy-start.3 = (f32[8,4096]{1,0:T(8,128)S(1)}, f32[8,4096]{1,0:T(8,128)}, u32[]{:S(2)}) copy-start(f32[8,4096]{1,0:T(8,128)} %rat_hbm.1) | copy-start | bytes 393220
  3.6 0.9 %copy-start.4 = (f32[8,4096]{1,0:T(8,128)S(1)}, f32[8,4096]{1,0:T(8,128)}, u32[]{:S(2)}) copy-start(f32[8,4096]{1,0:T(8,128)} %ret_hbm.1) | copy-start | bytes 393220
  4.5 0.9 %copy-start.5 = (f32[8,4096]{1,0:T(8,128)S(1)}, f32[8,4096]{1,0:T(8,128)}, u32[]{:S(2)}) copy-start(f32[8,4096]{1,0:T(8,128)} %wei_hbm.1) | copy-start | bytes 393220
  5.4 0.8 %copy-start.6 = (s32[4,4096]{1,0:T(4,128)S(1)}, s32[4,4096]{1,0:T(4,128)}, u32[]{:S(2)}) copy-start(s32[4,4096]{1,0:T(4,128)} %cor_hbm.1) | copy-start | bytes 196612
  6.3 0.8 %copy-start.7 = (f32[2,4096]{1,0:T(2,128)S(1)}, f32[2,4096]{1,0:T(2,128)}, u32[]{:S(2)}) copy-start(f32[2,4096]{1,0:T(2,128)} %str_hbm.1) | copy-start | bytes 98308
  7.0 0.8 %copy-start.8 = (f32[2,4096]{1,0:T(2,128)S(1)}, f32[2,4096]{1,0:T(2,128)}, u32[]{:S(2)}) copy-start(f32[2,4096]{1,0:T(2,128)} %she_hbm.1) | copy-start | bytes 98308
  7.8 0.7 %copy-start.9 = (s32[4,128]{1,0:T(4,128)S(1)}, s32[4,128]{1,0:T(4,128)}, u32[]{:S(2)}) copy-start(s32[4,128]{1,0:T(4,128)} %sha_hbm.1) | copy-start | bytes 6148

commit v2 on v1

--- a/solution.py
+++ b/solution.py
@@ -15,7 +15,8 @@
 WIDE = 256
 OWN_ROWS = 16
 ALL_ROWS = 18
-MAIN_BLOCK = 512
+GATHER_BLOCK = 2048
+MAIN_BLOCK = 1024
 SCATTER_BLOCK = 1024
 
 
@@ -127,7 +128,7 @@
     vel_hbm, adj_hbm, cor_hbm, sha_hbm, str_hbm, she_hbm, thi_hbm, rat_hbm, ret_hbm, wei_hbm,
     out,
     vel, adj, corners, shared, stretch, shear, thick, rate, ret, wei,
-    table, table8, low_send, low_own, gsend, grecv, lsend, lrecv,
+    table, late, hot, held, low_send, low_own, gsend, grecv, lsend, lrecv,
     fac, off, sc_send, sc_recv, en_send, en_recv,
     abuf, bbuf, acc,
     rs_send, rs_recv, gh_send, gh_recv, ag_send, ag_recv,
@@ -205,7 +206,7 @@
     row16 = iota((16, 128), 0)
     for j in range(4):
         ids = shared[j : j + 1, :]
-        sent = jnp.dot(table[0 : OWN_ROWS * 32], one_hot(ids & (WIDE - 1), WIDE), preferred_element_type=f32)
+        sent = jnp.dot(table[...], one_hot(ids & (WIDE - 1), WIDE), preferred_element_type=f32)
         sent = pick(ids >> 8, 32, sent, OWN_ROWS)
         gsend[j] = sent.astype(bf16)
         tops = jnp.zeros((16, 128), f32)
@@ -280,6 +281,19 @@
     def _():
         low_copy.start()
 
+    def gather_block(b, _):
+        c = lax.rem(b, 4)
+        at = pl.ds(pl.multiple_of(b // 4 * GATHER_BLOCK, GATHER_BLOCK), GATHER_BLOCK)
+        ids = corners[pl.ds(c, 1), at]
+        spot = one_hot(ids & (WIDE - 1), WIDE)
+        hot[c, :, at] = spot
+        held[c, :, at] = pick(ids >> 8, 32, jnp.dot(table[...], spot, preferred_element_type=f32), OWN_ROWS)
+        return 0
+
+    gathers = corners.shape[1] // GATHER_BLOCK * 4
+    loads[5].wait()
+    lax.fori_loop(0, gathers // 2, gather_block, 0)
+
     sc_recv[g] = sc_send[g]
     from_all(sc_send, sc_recv, sc_s, sc_r)
     running = jnp.zeros((per, WIDE), f32)
@@ -289,7 +303,8 @@
     to_all(en_send, en_recv, en_s, en_r)
     en_recv[g] = en_send[g]
 
-    for load in loads[5:]:
+    lax.fori_loop(gathers // 2, gathers, gather_block, 0)
+    for load in loads[6:]:
         load.wait()
 
     for j in range(4):
@@ -306,22 +321,21 @@
         low_copy.wait_recv()
 
     for i in range(2):
-        table[(OWN_ROWS + i) * 32 : (OWN_ROWS + i + 1) * 32] = jnp.concatenate([grecv[2 * i], grecv[2 * i + 1]], axis=1)
-    table8[0:64] = low_own[...]
+        late[i * 32 : (i + 1) * 32] = jnp.concatenate([grecv[2 * i], grecv[2 * i + 1]], axis=1)
+    late[64:128] = low_own[...]
     first = jnp.concatenate([lrecv[0], lrecv[1]], axis=1).astype(f32)[0:8]
     second = jnp.concatenate([lrecv[2], lrecv[3]], axis=1).astype(f32)[0:8]
     ghosts8 = first + pltpu.roll(second, 4, 0)
-    table8[64:80] = jnp.concatenate([ghosts8, jnp.zeros((8, WIDE), f32)], axis=0).astype(bf16)
+    late[128:144] = jnp.concatenate([ghosts8, jnp.zeros((8, WIDE), f32)], axis=0).astype(bf16)
 
     def main_block(b, _):
         at = pl.ds(pl.multiple_of(b * MAIN_BLOCK, MAIN_BLOCK), MAIN_BLOCK)
         upper, lowest = [], []
         for c in range(4):
-            ids = corners[c : c + 1, at]
-            row = ids >> 8
-            hot = one_hot(ids & (WIDE - 1), WIDE)
-            upper.append(pick(row, 32, jnp.dot(table[...], hot, preferred_element_type=f32), ALL_ROWS))
-            both = pick(row >> 1, 8, jnp.dot(table8[...], hot, preferred_element_type=f32), ALL_ROWS // 2)
+            row = corners[c : c + 1, at] >> 8
+            found = jnp.dot(late[...], hot[c, :, at], preferred_element_type=f32)
+            upper.append(jnp.where(row == 17, found[32:64], jnp.where(row == 16, found[0:32], held[c, :, at])))
+            both = pick(row >> 1, 8, found[64:136], ALL_ROWS // 2)
             lowest.append(jnp.where((row & 1) == 1, pltpu.roll(both, 4, 0), both))
         term = element_terms(upper, lowest, stretch[:, at], shear[:, at], thick[:, at], rate[:, at])
         abuf[:, at] = jnp.sum(fac[:, at] * term, axis=0, keepdims=True)
@@ -349,7 +363,7 @@
             ids = corners[c : c + 1, at]
             spread = jnp.where(place == (ids >> 8), value, 0.0).astype(bf16)
             part = lax.dot_general(
-                one_hot(ids & (WIDE - 1), WIDE), spread, (((1,), (1,)), ((), ())), preferred_element_type=f32
+                hot[c, :, at], spread, (((1,), (1,)), ((), ())), preferred_element_type=f32
             )
             out48 = part if out48 is None else out48 + part
         acc[...] += out48
@@ -443,11 +457,12 @@
     out = pl.pallas_call(
         functools.partial(kernel, layers, planes),
         out_shape=jax.ShapeDtypeStruct((32, 128), f32),
-        in_specs=[pl.BlockSpec(memory_space=pl.ANY)] * 10,
+        in_specs=[pl.BlockSpec(memory_space=pltpu.HBM)] * 10,
         out_specs=pl.BlockSpec(memory_space=pltpu.VMEM),
         scratch_shapes=[vmem(a.shape, a.dtype) for a in args]
         + [
-            vmem((ALL_ROWS * 32, WIDE), bf16), vmem((80, WIDE), bf16),
+            vmem((OWN_ROWS * 32, WIDE), bf16), vmem((144, WIDE), bf16),
+            vmem((4, WIDE, elems), bf16), vmem((4, 32, elems), f32),
             vmem((64, WIDE), bf16), vmem((64, WIDE), bf16),
             vmem((4, 32, 128), bf16), vmem((4, 32, 128), bf16),
             vmem((4, 16, 128), bf16), vmem((4, 16, 128), bf16),
@@ -461,7 +476,7 @@
             dma((10,)), dma, dma, dma((4,)), dma((4,)), dma((4,)), dma((4,)),
         ]
         + [dma((layers,)), dma((layers,)), dma((layers,)), dma((layers,)), dma((layers,)), dma((layers,)), dma((4,)), dma((4,)), dma((layers,)), dma((layers,))],
-        compiler_params=pltpu.CompilerParams(collective_id=0, has_side_effects=True, vmem_limit_bytes=40 << 20),
+        compiler_params=pltpu.CompilerParams(collective_id=0, has_side_effects=True, vmem_limit_bytes=60 << 20),
         name="ice_gradient",
     )(*args)
     return out.reshape(4096)

time: 55.6 us -> 42.6 us (0.77)
  local copies, waits for them, and re-layouts: 9.06 us -> 1.32 us
  Pallas kernels: 46.1 us -> 41.1 us
    unnamed x21 -> x1, local copies, waits for them, and re-layouts: 9.06 us -> 1.32 us
    pallas_call x1, Pallas kernels: 46.1 us -> 41.1 us  [shards(): pl.pallas_call(functools.partial(kernel, layers, planes), out_shape=jax.S...]
where the time goes in v2:
time: 42.6 us; the launch traced here: 42.4 us
  Pallas kernels  41.1 us (96%)
  local copies, waits for them, and re-layouts  1.32 us (3%)
    pallas_call x1, Pallas kernels, shards(): pl.pallas_call(functools.partial(kernel, layers, planes), out_shape=jax.S...  41.1 us
    unnamed x1, local copies, waits for them, and re-layouts  1.32 us

profile of v2, /device:TPU:7, one launch (start us, length us, event | category | flops | bytes accessed | tf_op | source)
XLA Modules:
  0.0 42.4 jit_solution(14704281409506380775)
XLA Ops:
  0.0 41.1 %ice_gradient.1 = f32[32,128]{1,0:T(8,128)} custom-call(bf16[2,8,4096]{2,1,0:T(8,128)(2,1)} %vel_hbm.1, bf16[2,8,4096]{2,1,0:T(8,128)(2,1)} %adj_hbm.1, s32[4,4096]{1,0:T(4,128)} %cor_hbm.1, s32[4,128]{1,0:T(4,128)} %sha_hbm.1, f32[2,4096]{1,0:T(2,128)} %str_hbm.1, f32[2,4096]{1,0:T(2,128)} %she_hbm.1, f32[8,4096]{1,0:T(8,128)} %thi_hbm.1, ...), custom_call_target="tpu_custom_call" | custom-call | tf_op jit(solution)/shard_map/ice_gradient/pallas_call | solution.py:457
  41.1 1.3 %copy.12 = f32[4096]{0:T(1024)} copy(f32[4096]{0:T(1024)} %bitcast.1) | data formatting | bytes 32768

commit v3 on v2

--- a/solution.py
+++ b/solution.py
@@ -13,11 +13,16 @@
 GAUSS = 1.0 / math.sqrt(3.0)
 MESH = pl.DeviceIdType.MESH
 WIDE = 256
+HALF = 2048
 OWN_ROWS = 16
 ALL_ROWS = 18
-GATHER_BLOCK = 2048
+GATHER_BLOCK = 4096
 MAIN_BLOCK = 1024
-SCATTER_BLOCK = 1024
+SCATTER_BLOCK = 4096
+
+
+def far_first(k, count):
+    return count // 2 + (k + 1) // 2 * (2 * lax.rem(k, 2) - 1)
 
 
 def iota(shape, axis):
@@ -26,6 +31,17 @@
 
 def one_hot(low, width):
     return (iota((width, low.shape[1]), 0) == low).astype(jnp.float32).astype(jnp.bfloat16)
+
+
+def place_of(ids):
+    owned = ids < 2 * HALF
+    row = jnp.where(owned, (ids >> 7) & 15, ids >> 8)
+    spot = jnp.where(owned, (ids & 127) | ((ids >> 4) & 128), ids & 255)
+    return row, spot
+
+
+def owned_row(ref, lead, i):
+    return jnp.concatenate([ref[lead, :, i * 128 : (i + 1) * 128], ref[lead, :, HALF + i * 128 : HALF + (i + 1) * 128]], axis=1)
 
 
 def pick(row, size, table, count):
@@ -128,11 +144,11 @@
     vel_hbm, adj_hbm, cor_hbm, sha_hbm, str_hbm, she_hbm, thi_hbm, rat_hbm, ret_hbm, wei_hbm,
     out,
     vel, adj, corners, shared, stretch, shear, thick, rate, ret, wei,
-    table, late, hot, held, low_send, low_own, gsend, grecv, lsend, lrecv,
+    table, late, late8, hot, held, rows, low_send, low_own, gsend, grecv, lsend, lrecv,
     fac, off, sc_send, sc_recv, en_send, en_recv,
-    abuf, bbuf, acc,
-    rs_send, rs_recv, gh_send, gh_recv, ag_send, ag_recv,
-    in_sem, low_s, low_r, g_s, g_r, l_s, l_r, sc_s, sc_r, en_s, en_r, rs_s, rs_r, gh_s, gh_r, ag_s, ag_r,
+    abuf, bbuf,
+    gh_send, gh_recv, pair_send, pair_recv, all_recv, done,
+    in_sem, low_s, low_r, g_s, g_r, l_s, l_r, sc_s, sc_r, en_s, en_r, gh_s, gh_r, pair_s, pair_r, all_s, all_r, last_s, last_r,
 ):
     g, p = lax.axis_index("layer"), lax.axis_index("plane")
     per = OWN_ROWS // layers
@@ -188,17 +204,14 @@
     loads[0].wait()
     loads[1].wait()
     for i in range(OWN_ROWS):
-        at = slice(i * WIDE, (i + 1) * WIDE)
-        table[i * 32 : (i + 1) * 32] = jnp.concatenate(
-            [vel[0, :, at], vel[1, :, at], adj[0, :, at], adj[1, :, at]], axis=0
-        )
+        table[i * 32 : (i + 1) * 32] = jnp.concatenate([owned_row(f, k, i) for f in (vel, adj) for k in range(2)], axis=0)
     row8 = iota((8, WIDE), 0)
     pieces = []
     for i in range(0, OWN_ROWS, 2):
         piece = jnp.zeros((8, WIDE), f32)
         for half in range(2):
             for comp in range(4):
-                level = (vel, adj)[comp // 2][comp % 2, :, (i + half) * WIDE : (i + half + 1) * WIDE].astype(f32)
+                level = owned_row((vel, adj)[comp // 2], comp % 2, i + half).astype(f32)
                 piece = jnp.where(row8 == half * 4 + comp, level[0:1], piece)
         pieces.append(piece)
     low_send[...] = jnp.concatenate(pieces, axis=0).astype(bf16)
@@ -206,8 +219,9 @@
     row16 = iota((16, 128), 0)
     for j in range(4):
         ids = shared[j : j + 1, :]
-        sent = jnp.dot(table[...], one_hot(ids & (WIDE - 1), WIDE), preferred_element_type=f32)
-        sent = pick(ids >> 8, 32, sent, OWN_ROWS)
+        row, spot = place_of(ids)
+        sent = jnp.dot(table[...], one_hot(spot, WIDE), preferred_element_type=f32)
+        sent = pick(row, 32, sent, OWN_ROWS)
         gsend[j] = sent.astype(bf16)
         tops = jnp.zeros((16, 128), f32)
         for comp in range(4):
@@ -233,28 +247,28 @@
             src_ref=src, dst_ref=dst, send_sem=s, recv_sem=r, device_id=(layer, plane), device_id_type=MESH
         )
 
-    def to_all(send, recv, s, r, same=False):
+    def to_all(send, recv, s, r):
         def copy(i):
-            return remote(send if same else send.at[i], recv.at[g], s.at[i], r.at[g], i, p)
+            return remote(send.at[i], recv.at[g], s.at[i], r.at[g], i, p)
 
         def start(k, _):
-            copy(lax.rem(g + k, layers)).start()
+            copy(lax.rem(g + far_first(k, layers), layers)).start()
             return 0
 
-        lax.fori_loop(1, layers, start, 0)
-
-    def from_all(send, recv, s, r, same=False):
+        lax.fori_loop(0, layers - 1, start, 0)
+
+    def from_all(send, recv, s, r):
         def wait(k, _):
             i = lax.rem(g + k, layers)
-            remote(send if same else send.at[i], recv.at[i], s.at[i], r.at[i], i, p).wait_recv()
+            remote(send.at[i], recv.at[i], s.at[i], r.at[i], i, p).wait_recv()
             return 0
 
         lax.fori_loop(1, layers, wait, 0)
 
-    def sent_all(send, recv, s, r, same=False):
+    def sent_all(send, recv, s, r):
         def wait(k, _):
             i = lax.rem(g + k, layers)
-            remote(send if same else send.at[i], recv.at[i], s.at[i], r.at[i], i, p).wait_send()
+            remote(send.at[i], recv.at[i], s.at[i], r.at[i], i, p).wait_send()
             return 0
 
         lax.fori_loop(1, layers, wait, 0)
@@ -284,15 +298,16 @@
     def gather_block(b, _):
         c = lax.rem(b, 4)
         at = pl.ds(pl.multiple_of(b // 4 * GATHER_BLOCK, GATHER_BLOCK), GATHER_BLOCK)
-        ids = corners[pl.ds(c, 1), at]
-        spot = one_hot(ids & (WIDE - 1), WIDE)
+        row, spot = place_of(corners[pl.ds(c, 1), at])
+        spot = one_hot(spot, WIDE)
+        rows[pl.ds(c, 1), at] = row
         hot[c, :, at] = spot
-        held[c, :, at] = pick(ids >> 8, 32, jnp.dot(table[...], spot, preferred_element_type=f32), OWN_ROWS)
+        held[c, :, at] = pick(row, 32, jnp.dot(table[...], spot, preferred_element_type=f32), OWN_ROWS)
         return 0
 
     gathers = corners.shape[1] // GATHER_BLOCK * 4
     loads[5].wait()
-    lax.fori_loop(0, gathers // 2, gather_block, 0)
+    lax.fori_loop(0, gathers, gather_block, 0)
 
     sc_recv[g] = sc_send[g]
     from_all(sc_send, sc_recv, sc_s, sc_r)
@@ -303,7 +318,6 @@
     to_all(en_send, en_recv, en_s, en_r)
     en_recv[g] = en_send[g]
 
-    lax.fori_loop(gathers // 2, gathers, gather_block, 0)
     for load in loads[6:]:
         load.wait()
 
@@ -322,20 +336,26 @@
 
     for i in range(2):
         late[i * 32 : (i + 1) * 32] = jnp.concatenate([grecv[2 * i], grecv[2 * i + 1]], axis=1)
-    late[64:128] = low_own[...]
+    late8[0:64] = low_own[...]
     first = jnp.concatenate([lrecv[0], lrecv[1]], axis=1).astype(f32)[0:8]
     second = jnp.concatenate([lrecv[2], lrecv[3]], axis=1).astype(f32)[0:8]
     ghosts8 = first + pltpu.roll(second, 4, 0)
-    late[128:144] = jnp.concatenate([ghosts8, jnp.zeros((8, WIDE), f32)], axis=0).astype(bf16)
+    late8[64:80] = jnp.concatenate([ghosts8, jnp.zeros((8, WIDE), f32)], axis=0).astype(bf16)
 
     def main_block(b, _):
         at = pl.ds(pl.multiple_of(b * MAIN_BLOCK, MAIN_BLOCK), MAIN_BLOCK)
         upper, lowest = [], []
         for c in range(4):
-            row = corners[c : c + 1, at] >> 8
-            found = jnp.dot(late[...], hot[c, :, at], preferred_element_type=f32)
-            upper.append(jnp.where(row == 17, found[32:64], jnp.where(row == 16, found[0:32], held[c, :, at])))
-            both = pick(row >> 1, 8, found[64:136], ALL_ROWS // 2)
+            row = rows[c : c + 1, at]
+            if c == 0:
+                found = jnp.dot(late[...], hot[c, :, at], preferred_element_type=f32)
+                upper.append(jnp.where(row == 17, found[32:64], jnp.where(row == 16, found[0:32], held[c, :, at])))
+                found = jnp.dot(late8[...], hot[c, :, at], preferred_element_type=f32)
+                both = pick(row >> 1, 8, found, ALL_ROWS // 2)
+            else:
+                upper.append(held[c, :, at])
+                found = jnp.dot(late8[0:64], hot[c, :, at], preferred_element_type=f32)
+                both = pick(row >> 1, 8, found, OWN_ROWS // 2)
             lowest.append(jnp.where((row & 1) == 1, pltpu.roll(both, 4, 0), both))
         term = element_terms(upper, lowest, stretch[:, at], shear[:, at], thick[:, at], rate[:, at])
         abuf[:, at] = jnp.sum(fac[:, at] * term, axis=0, keepdims=True)
@@ -350,88 +370,94 @@
             at = slice((i * per + k) * WIDE, (i * per + k + 1) * WIDE)
             abuf[:, at] = 0.25 * (abuf[:, at] * en_recv[i, k : k + 1, :] + bbuf[:, at])
 
-    acc[...] = jnp.zeros(acc.shape, f32)
-
-    def scatter_block(b, _):
-        at = pl.ds(pl.multiple_of(b * SCATTER_BLOCK, SCATTER_BLOCK), SCATTER_BLOCK)
-        row48 = iota((48, SCATTER_BLOCK), 0)
-        high, low = split_bf16(abuf[:, at])
-        value = jnp.where(row48 < 24, high, low)
-        place = jnp.where(row48 < 24, row48, row48 - 24)
-        out48 = None
-        for c in range(4):
-            ids = corners[c : c + 1, at]
-            spread = jnp.where(place == (ids >> 8), value, 0.0).astype(bf16)
-            part = lax.dot_general(
-                hot[c, :, at], spread, (((1,), (1,)), ((), ())), preferred_element_type=f32
-            )
-            out48 = part if out48 is None else out48 + part
-        acc[...] += out48
-        return 0
-
-    lax.fori_loop(0, corners.shape[1] // SCATTER_BLOCK, scatter_block, 0)
-    nodes = acc[...].T
-    nodes = nodes[0:24] + nodes[24:48]
-    for i in range(layers):
-        for k in range(per):
-            lo = i * per + k
-            rs_send[i, 2 * k : 2 * k + 1, :] = nodes[lo : lo + 1, 0:128]
-            rs_send[i, 2 * k + 1 : 2 * k + 2, :] = nodes[lo : lo + 1, 128:256]
-    for j in range(4):
-        gh_send[j] = nodes[OWN_ROWS + j // 2 : OWN_ROWS + j // 2 + 1, (j % 2) * 128 : (j % 2 + 1) * 128]
+    def scatter(c, count):
+        def block(b, total):
+            at = slice(b * SCATTER_BLOCK, (b + 1) * SCATTER_BLOCK)
+            line = iota((2 * count, SCATTER_BLOCK), 0)
+            high, low = split_bf16(abuf[:, at])
+            value = jnp.where(line < count, high, low)
+            place = jnp.where(line < count, line, line - count)
+            spread = jnp.where(place == rows[c : c + 1, at], value, 0.0).astype(bf16)
+            return total + lax.dot_general(hot[c, :, at], spread, (((1,), (1,)), ((), ())), preferred_element_type=f32)
+
+        total = block(0, jnp.zeros((WIDE, 2 * count), f32)).T
+        return total[0:count] + total[count : 2 * count]
 
     def ghost_sum(j):
         return remote(gh_send.at[j], gh_recv.at[3 - j], gh_s.at[j], gh_r.at[3 - j], g, p + OFFSETS[j])
 
+    nodes = scatter(0, 24)
+    for j in range(4):
+        gh_send[j] = nodes[OWN_ROWS + j // 2 : OWN_ROWS + j // 2 + 1, (j % 2) * 128 : (j % 2 + 1) * 128]
     for j in range(4):
         @pl.when(valid[j])
         def _():
             ghost_sum(j).start()
-    to_all(rs_send, rs_recv, rs_s, rs_r)
-    rs_recv[g] = rs_send[g]
-
-    hots, spots = [], []
-    row64 = iota((64, 128), 0) & 31
+    owned = nodes[0:OWN_ROWS]
+    for c in range(1, 4):
+        owned = owned + scatter(c, OWN_ROWS)
+    owned = jnp.concatenate([owned[:, 0:128], owned[:, 128:256]], axis=0)
+
+    for j in range(4):
+        @pl.when(valid[j])
+        def _():
+            remote(gh_send.at[j], gh_recv.at[j], gh_s.at[j], gh_r.at[j], g, p + OFFSETS[j]).wait_recv()
+    row64 = iota((64, 128), 0)
+    added = None
     for d in range(4):
         ids = shared[d : d + 1, :]
-        hots.append(one_hot(ids & 127, 128))
-        spots.append(row64 == (ids >> 7))
-
-    for j in range(4):
-        @pl.when(valid[j])
-        def _():
-            remote(gh_send.at[j], gh_recv.at[j], gh_s.at[j], gh_r.at[j], g, p + OFFSETS[j]).wait_recv()
-    from_all(rs_send, rs_recv, rs_s, rs_r)
-    total = rs_recv[0]
-    for i in range(1, layers):
-        total = total + rs_recv[i]
-    ag_send[0 : 2 * per] = total
-    for d in range(4):
-        ag_send[2 * per + d : 2 * per + d + 1] = gh_recv[d]
-    spare = ag_send.shape[0] - 2 * per - 4
-    if spare:
-        ag_send[2 * per + 4 :] = jnp.zeros((spare, 128), f32)
-    to_all(ag_send, ag_recv, ag_s, ag_r, same=True)
-    ag_recv[g] = ag_send[...]
-    from_all(ag_send, ag_recv, ag_s, ag_r, same=True)
-
-    arrived = ag_recv[0]
-    for i in range(1, layers):
-        arrived = arrived + ag_recv[i]
-    result = jnp.concatenate([ag_recv[i, 0 : 2 * per, :] for i in range(layers)], axis=0)
-    added = None
-    half64 = iota((64, 128), 0) < 32
-    for d in range(4):
-        high, low = split_bf16(arrived[2 * per + d : 2 * per + d + 1])
-        spread = jnp.where(spots[d], jnp.where(half64, high, low), 0.0).astype(bf16)
-        part = lax.dot_general(spread, hots[d], (((1,), (1,)), ((), ())), preferred_element_type=f32)
+        high, low = split_bf16(gh_recv[d])
+        spread = jnp.where((row64 & 31) == (ids >> 7), jnp.where(row64 < 32, high, low), 0.0).astype(bf16)
+        part = lax.dot_general(spread, one_hot(ids & 127, 128), (((1,), (1,)), ((), ())), preferred_element_type=f32)
         added = part if added is None else added + part
-    out[...] = result + (added[0:32] + added[32:64])
-
+    owned = owned + (added[0:32] + added[32:64])
+
+    core, chip, chips = lax.rem(g, 2), g // 2, layers // 2
+    mate = g + 1 - 2 * core
+    pair_send[0] = owned[0:16]
+    pair_send[1] = owned[16:32]
+    pair = remote(pair_send.at[1 - core], pair_recv, pair_s, pair_r, mate, p)
+    pair.start()
+    pair.wait_recv()
+    all_recv[chip] = pair_send[core] + pair_recv[...]
+
+    def over_chips(k):
+        i = lax.rem(chip + k, chips)
+        return remote(all_recv.at[chip], all_recv.at[chip], all_s.at[i], all_r.at[chip], 2 * i + core, p)
+
+    def from_chip(k):
+        i = lax.rem(chip + k, chips)
+        return remote(all_recv.at[chip], all_recv.at[i], all_s.at[i], all_r.at[i], 2 * i + core, p)
+
+    def start_chip(k, _):
+        over_chips(far_first(k, chips)).start()
+        return 0
+
+    def wait_chip(k, _):
+        from_chip(k).wait_recv()
+        return 0
+
+    lax.fori_loop(0, chips - 1, start_chip, 0)
+    lax.fori_loop(1, chips, wait_chip, 0)
+    total = all_recv[0]
+    for i in range(1, chips):
+        total = total + all_recv[i]
+    done[core] = total
+    last = remote(done.at[core], done.at[core], last_s, last_r, mate, p)
+    last.start()
+    remote(done.at[core], done.at[1 - core], last_s, last_r, mate, p).wait_recv()
+    out[0:16] = done[0]
+    out[16:32] = done[1]
+
+    def sent_chip(k, _):
+        over_chips(k).wait_send()
+        return 0
+
+    lax.fori_loop(1, chips, sent_chip, 0)
+    pair.wait_send()
+    last.wait_send()
     sent_all(sc_send, sc_recv, sc_s, sc_r)
     sent_all(en_send, en_recv, en_s, en_r)
-    sent_all(rs_send, rs_recv, rs_s, rs_r)
-    sent_all(ag_send, ag_recv, ag_s, ag_r, same=True)
     for j in range(4):
         @pl.when(valid[j])
         def _():
@@ -451,7 +477,6 @@
     velocity, adjoint, corners, shared, stretch, shear_part, thickness, rate_factor, retention, weight = args
     per = OWN_ROWS // layers
     elems = corners.shape[1]
-    gathered = -(-(2 * per + 4) // 8) * 8
     f32, bf16 = jnp.float32, jnp.bfloat16
     vmem, dma = pltpu.VMEM, pltpu.SemaphoreType.DMA
     out = pl.pallas_call(
@@ -461,21 +486,21 @@
         out_specs=pl.BlockSpec(memory_space=pltpu.VMEM),
         scratch_shapes=[vmem(a.shape, a.dtype) for a in args]
         + [
-            vmem((OWN_ROWS * 32, WIDE), bf16), vmem((144, WIDE), bf16),
-            vmem((4, WIDE, elems), bf16), vmem((4, 32, elems), f32),
+            vmem((OWN_ROWS * 32, WIDE), bf16), vmem((64, WIDE), bf16), vmem((80, WIDE), bf16),
+            vmem((4, WIDE, elems), bf16), vmem((4, 32, elems), f32), vmem((4, elems), jnp.int32),
             vmem((64, WIDE), bf16), vmem((64, WIDE), bf16),
             vmem((4, 32, 128), bf16), vmem((4, 32, 128), bf16),
             vmem((4, 16, 128), bf16), vmem((4, 16, 128), bf16),
             vmem((8, elems), f32), vmem((8, elems), f32),
             vmem((layers, 2 * per, WIDE), f32), vmem((layers, 2 * per, WIDE), f32),
             vmem((layers, per, WIDE), f32), vmem((layers, per, WIDE), f32),
-            vmem((1, elems), f32), vmem((1, elems), f32), vmem((WIDE, 48), f32),
-            vmem((layers, 2 * per, 128), f32), vmem((layers, 2 * per, 128), f32),
+            vmem((1, elems), f32), vmem((1, elems), f32),
             vmem((4, 1, 128), f32), vmem((4, 1, 128), f32),
-            vmem((gathered, 128), f32), vmem((layers, gathered, 128), f32),
+            vmem((2, 16, 128), f32), vmem((16, 128), f32), vmem((layers // 2, 16, 128), f32), vmem((2, 16, 128), f32),
             dma((10,)), dma, dma, dma((4,)), dma((4,)), dma((4,)), dma((4,)),
         ]
-        + [dma((layers,)), dma((layers,)), dma((layers,)), dma((layers,)), dma((layers,)), dma((layers,)), dma((4,)), dma((4,)), dma((layers,)), dma((layers,))],
+        + [dma((layers,)), dma((layers,)), dma((layers,)), dma((layers,)), dma((4,)), dma((4,)), dma, dma]
+        + [dma((layers // 2,)), dma((layers // 2,)), dma, dma],
         compiler_params=pltpu.CompilerParams(collective_id=0, has_side_effects=True, vmem_limit_bytes=60 << 20),
         name="ice_gradient",
     )(*args)

time: 42.6 us -> 39.9 us (0.937); the launches traced: 42.4 us -> 39.2 us
  Pallas kernels: 41.1 us -> 37.9 us
    pallas_call x1, Pallas kernels: 41.1 us -> 37.9 us  [shards(): pl.pallas_call(functools.partial(kernel, layers, planes), out_shape=jax.S...]
where the time goes in v3:
time: 39.9 us; the launch traced here: 39.2 us
  Pallas kernels  37.9 us (95%)
  local copies, waits for them, and re-layouts  1.32 us (3%)
    pallas_call x1, Pallas kernels, shards(): pl.pallas_call(functools.partial(kernel, layers, planes), out_shape=jax.S...  37.9 us
    unnamed x1, local copies, waits for them, and re-layouts  1.32 us

profile of v3, /device:TPU:7, one launch (start us, length us, event | category | flops | bytes accessed | tf_op | source)
XLA Modules:
  0.0 39.2 jit_solution(8944598857013882709)
XLA Ops:
  0.0 37.9 %ice_gradient.1 = f32[32,128]{1,0:T(8,128)} custom-call(bf16[2,8,4096]{2,1,0:T(8,128)(2,1)} %vel_hbm.1, bf16[2,8,4096]{2,1,0:T(8,128)(2,1)} %adj_hbm.1, s32[4,4096]{1,0:T(4,128)} %cor_hbm.1, s32[4,128]{1,0:T(4,128)} %sha_hbm.1, f32[2,4096]{1,0:T(2,128)} %str_hbm.1, f32[2,4096]{1,0:T(2,128)} %she_hbm.1, f32[8,4096]{1,0:T(8,128)} %thi_hbm.1, ...), custom_call_target="tpu_custom_call" | custom-call | tf_op jit(solution)/shard_map/ice_gradient/pallas_call | solution.py:482
  37.9 1.3 %copy.12 = f32[4096]{0:T(1024)} copy(f32[4096]{0:T(1024)} %bitcast.1) | data formatting | bytes 32768

commit v4 on v3

--- a/solution.py
+++ b/solution.py
@@ -16,8 +16,7 @@
 HALF = 2048
 OWN_ROWS = 16
 ALL_ROWS = 18
-GATHER_BLOCK = 4096
-MAIN_BLOCK = 1024
+MAIN_BLOCK = 512
 SCATTER_BLOCK = 4096
 
 
@@ -144,11 +143,11 @@
     vel_hbm, adj_hbm, cor_hbm, sha_hbm, str_hbm, she_hbm, thi_hbm, rat_hbm, ret_hbm, wei_hbm,
     out,
     vel, adj, corners, shared, stretch, shear, thick, rate, ret, wei,
-    table, late, late8, hot, held, rows, low_send, low_own, gsend, grecv, lsend, lrecv,
+    table, late, late8, hot, held, rows, low0, top_send, top_recv, low_send, low_own, gsend, grecv, lsend, lrecv,
     fac, off, sc_send, sc_recv, en_send, en_recv,
     abuf, bbuf,
     gh_send, gh_recv, pair_send, pair_recv, all_recv, done,
-    in_sem, low_s, low_r, g_s, g_r, l_s, l_r, sc_s, sc_r, en_s, en_r, gh_s, gh_r, pair_s, pair_r, all_s, all_r, last_s, last_r,
+    in_sem, low_s, low_r, top_s, top_r, g_s, g_r, l_s, l_r, sc_s, sc_r, en_s, en_r, gh_s, gh_r, pair_s, pair_r, all_s, all_r, last_s, last_r,
 ):
     g, p = lax.axis_index("layer"), lax.axis_index("plane")
     per = OWN_ROWS // layers
@@ -174,6 +173,7 @@
     def _():
         low_own[...] = jnp.zeros(low_own.shape, bf16)
         lrecv[...] = jnp.zeros(lrecv.shape, bf16)
+        top_recv[...] = jnp.zeros(top_recv.shape, bf16)
 
     barrier = pltpu.get_barrier_semaphore()
 
@@ -282,6 +282,7 @@
     low_copy = remote(low_send, low_own, low_s, low_r, g - 1, p)
 
     to_all(sc_send, sc_recv, sc_s, sc_r)
+
     for j in range(4):
         @pl.when(valid[j])
         def _():
@@ -295,28 +296,41 @@
     def _():
         low_copy.start()
 
-    def gather_block(b, _):
-        c = lax.rem(b, 4)
-        at = pl.ds(pl.multiple_of(b // 4 * GATHER_BLOCK, GATHER_BLOCK), GATHER_BLOCK)
-        row, spot = place_of(corners[pl.ds(c, 1), at])
+    def top_copy(i):
+        return remote(top_send.at[i], top_recv.at[i], top_s.at[i], top_r.at[i], g - 1, p)
+
+    def enter():
+        sc_recv[g] = sc_send[g]
+        from_all(sc_send, sc_recv, sc_s, sc_r)
+        running = jnp.zeros((per, WIDE), f32)
+        for i in range(layers):
+            en_send[i] = running
+            running = sc_recv[i, 0:per, :] * running + sc_recv[i, per : 2 * per, :]
+        to_all(en_send, en_recv, en_s, en_r)
+        en_recv[g] = en_send[g]
+
+    def gather(b, _):
+        @pl.when(b == 3)
+        def _():
+            enter()
+
+        c = lax.rem(b + 1, 4)
+        row, spot = place_of(corners[pl.ds(c, 1), :])
         spot = one_hot(spot, WIDE)
-        rows[pl.ds(c, 1), at] = row
-        hot[c, :, at] = spot
-        held[c, :, at] = pick(row, 32, jnp.dot(table[...], spot, preferred_element_type=f32), OWN_ROWS)
+        rows[pl.ds(c, 1), :] = row
+        hot[c] = spot
+        found = pick(row, 32, jnp.dot(table[...], spot, preferred_element_type=f32), OWN_ROWS)
+        held[c] = found
+
+        @pl.when(jnp.logical_and(b < 3, up))
+        def _():
+            top_send[b] = jnp.concatenate([found[8 * k : 8 * k + 1] for k in range(4)], axis=0).astype(bf16)
+            top_copy(b).start()
+
         return 0
 
-    gathers = corners.shape[1] // GATHER_BLOCK * 4
     loads[5].wait()
-    lax.fori_loop(0, gathers, gather_block, 0)
-
-    sc_recv[g] = sc_send[g]
-    from_all(sc_send, sc_recv, sc_s, sc_r)
-    running = jnp.zeros((per, WIDE), f32)
-    for i in range(layers):
-        en_send[i] = running
-        running = sc_recv[i, 0:per, :] * running + sc_recv[i, per : 2 * per, :]
-    to_all(en_send, en_recv, en_s, en_r)
-    en_recv[g] = en_send[g]
+    lax.fori_loop(0, 4, gather, 0)
 
     for load in loads[6:]:
         load.wait()
@@ -342,21 +356,24 @@
     ghosts8 = first + pltpu.roll(second, 4, 0)
     late8[64:80] = jnp.concatenate([ghosts8, jnp.zeros((8, WIDE), f32)], axis=0).astype(bf16)
 
+    row = rows[0:1, :]
+    found = jnp.dot(late[...], hot[0], preferred_element_type=f32)
+    held[0] = jnp.where(row == 17, found[32:64], jnp.where(row == 16, found[0:32], held[0]))
+    both = pick(row >> 1, 8, jnp.dot(late8[...], hot[0], preferred_element_type=f32), ALL_ROWS // 2)
+    low0[...] = jnp.where((row & 1) == 1, pltpu.roll(both, 4, 0), both)
+
+    for i in range(3):
+        @pl.when(down)
+        def _():
+            top_copy(i).wait_recv()
+
     def main_block(b, _):
         at = pl.ds(pl.multiple_of(b * MAIN_BLOCK, MAIN_BLOCK), MAIN_BLOCK)
-        upper, lowest = [], []
-        for c in range(4):
-            row = rows[c : c + 1, at]
-            if c == 0:
-                found = jnp.dot(late[...], hot[c, :, at], preferred_element_type=f32)
-                upper.append(jnp.where(row == 17, found[32:64], jnp.where(row == 16, found[0:32], held[c, :, at])))
-                found = jnp.dot(late8[...], hot[c, :, at], preferred_element_type=f32)
-                both = pick(row >> 1, 8, found, ALL_ROWS // 2)
-            else:
-                upper.append(held[c, :, at])
-                found = jnp.dot(late8[0:64], hot[c, :, at], preferred_element_type=f32)
-                both = pick(row >> 1, 8, found, OWN_ROWS // 2)
-            lowest.append(jnp.where((row & 1) == 1, pltpu.roll(both, 4, 0), both))
+        upper = [held[c, :, at] for c in range(4)]
+        lowest = [low0[:, at]]
+        for i in range(3):
+            level = top_recv[i, :, at].astype(f32)
+            lowest.append(jnp.concatenate([level, level], axis=0))
         term = element_terms(upper, lowest, stretch[:, at], shear[:, at], thick[:, at], rate[:, at])
         abuf[:, at] = jnp.sum(fac[:, at] * term, axis=0, keepdims=True)
         bbuf[:, at] = jnp.sum(off[:, at] * term, axis=0, keepdims=True)
@@ -438,6 +455,25 @@
         return 0
 
     lax.fori_loop(0, chips - 1, start_chip, 0)
+    sent_all(sc_send, sc_recv, sc_s, sc_r)
+    sent_all(en_send, en_recv, en_s, en_r)
+    pair.wait_send()
+    for j in range(4):
+        @pl.when(valid[j])
+        def _():
+            ghost(j).wait_send()
+            ghost_sum(j).wait_send()
+
+        @pl.when(jnp.logical_and(valid[j], up))
+        def _():
+            low_ghost(j).wait_send()
+
+    @pl.when(up)
+    def _():
+        low_copy.wait_send()
+        for i in range(3):
+            top_copy(i).wait_send()
+
     lax.fori_loop(1, chips, wait_chip, 0)
     total = all_recv[0]
     for i in range(1, chips):
@@ -454,23 +490,7 @@
         return 0
 
     lax.fori_loop(1, chips, sent_chip, 0)
-    pair.wait_send()
     last.wait_send()
-    sent_all(sc_send, sc_recv, sc_s, sc_r)
-    sent_all(en_send, en_recv, en_s, en_r)
-    for j in range(4):
-        @pl.when(valid[j])
-        def _():
-            ghost(j).wait_send()
-            ghost_sum(j).wait_send()
-
-        @pl.when(jnp.logical_and(valid[j], up))
-        def _():
-            low_ghost(j).wait_send()
-
-    @pl.when(up)
-    def _():
-        low_copy.wait_send()
 
 
 def shards(layers, planes, *args):
@@ -487,7 +507,8 @@
         scratch_shapes=[vmem(a.shape, a.dtype) for a in args]
         + [
             vmem((OWN_ROWS * 32, WIDE), bf16), vmem((64, WIDE), bf16), vmem((80, WIDE), bf16),
-            vmem((4, WIDE, elems), bf16), vmem((4, 32, elems), f32), vmem((4, elems), jnp.int32),
+            vmem((4, WIDE, elems), bf16), vmem((4, 32, elems), f32), vmem((4, elems), jnp.int32), vmem((8, elems), f32),
+            vmem((3, 4, elems), bf16), vmem((3, 4, elems), bf16),
             vmem((64, WIDE), bf16), vmem((64, WIDE), bf16),
             vmem((4, 32, 128), bf16), vmem((4, 32, 128), bf16),
             vmem((4, 16, 128), bf16), vmem((4, 16, 128), bf16),
@@ -497,7 +518,7 @@
             vmem((1, elems), f32), vmem((1, elems), f32),
             vmem((4, 1, 128), f32), vmem((4, 1, 128), f32),
             vmem((2, 16, 128), f32), vmem((16, 128), f32), vmem((layers // 2, 16, 128), f32), vmem((2, 16, 128), f32),
-            dma((10,)), dma, dma, dma((4,)), dma((4,)), dma((4,)), dma((4,)),
+            dma((10,)), dma, dma, dma((3,)), dma((3,)), dma((4,)), dma((4,)), dma((4,)), dma((4,)),
         ]
         + [dma((layers,)), dma((layers,)), dma((layers,)), dma((layers,)), dma((4,)), dma((4,)), dma, dma]
         + [dma((layers // 2,)), dma((layers // 2,)), dma, dma],

time: 39.9 us -> 38.8 us (0.972)
  Pallas kernels: 37.9 us -> 37 us
    pallas_call x1, Pallas kernels: 37.9 us -> 37 us  [shards(): pl.pallas_call(functools.partial(kernel, layers, planes), out_shape=jax.S...]
where the time goes in v4:
time: 38.8 us; the launch traced here: 38.3 us
  Pallas kernels  37 us (95%)
  local copies, waits for them, and re-layouts  1.32 us (3%)
    pallas_call x1, Pallas kernels, shards(): pl.pallas_call(functools.partial(kernel, layers, planes), out_shape=jax.S...  37 us
    unnamed x1, local copies, waits for them, and re-layouts  1.32 us

profile of v4, /device:TPU:7, one launch (start us, length us, event | category | flops | bytes accessed | tf_op | source)
XLA Modules:
  0.0 38.3 jit_solution(13562218516952553430)
XLA Ops:
  0.0 37.0 %ice_gradient.1 = f32[32,128]{1,0:T(8,128)} custom-call(bf16[2,8,4096]{2,1,0:T(8,128)(2,1)} %vel_hbm.1, bf16[2,8,4096]{2,1,0:T(8,128)(2,1)} %adj_hbm.1, s32[4,4096]{1,0:T(4,128)} %cor_hbm.1, s32[4,128]{1,0:T(4,128)} %sha_hbm.1, f32[2,4096]{1,0:T(2,128)} %str_hbm.1, f32[2,4096]{1,0:T(2,128)} %she_hbm.1, f32[8,4096]{1,0:T(8,128)} %thi_hbm.1, ...), custom_call_target="tpu_custom_call" | custom-call | tf_op jit(solution)/shard_map/ice_gradient/pallas_call | solution.py:502
  37.0 1.3 %copy.12 = f32[4096]{0:T(1024)} copy(f32[4096]{0:T(1024)} %bitcast.1) | data formatting | bytes 32768

commit v5 on v4

--- a/solution.py
+++ b/solution.py
@@ -167,7 +167,8 @@
         def _():
             grecv[d] = jnp.zeros(grecv.shape[1:], bf16)
             lrecv[d] = jnp.zeros(lrecv.shape[1:], bf16)
-            gh_recv[d] = jnp.zeros(gh_recv.shape[1:], f32)
+            gh_recv[0, d] = jnp.zeros(gh_recv.shape[2:], f32)
+            gh_recv[1, d] = jnp.zeros(gh_recv.shape[2:], f32)
 
     @pl.when(jnp.logical_not(down))
     def _():
@@ -400,8 +401,15 @@
         total = block(0, jnp.zeros((WIDE, 2 * count), f32)).T
         return total[0:count] + total[count : 2 * count]
 
-    def ghost_sum(j):
-        return remote(gh_send.at[j], gh_recv.at[3 - j], gh_s.at[j], gh_r.at[3 - j], g, p + OFFSETS[j])
+    core, chip, chips = lax.rem(g, 2), g // 2, layers // 2
+    mate = g + 1 - 2 * core
+
+    def ghost_sum(j, other):
+        to = mate if other else g
+        return remote(gh_send.at[j], gh_recv.at[core, 3 - j], gh_s.at[other, j], gh_r.at[core, 3 - j], to, p + OFFSETS[j])
+
+    def ghost_from(j, k):
+        return remote(gh_send.at[j], gh_recv.at[k, j], gh_s.at[0, j], gh_r.at[k, j], g, p + OFFSETS[j])
 
     nodes = scatter(0, 24)
     for j in range(4):
@@ -409,34 +417,33 @@
     for j in range(4):
         @pl.when(valid[j])
         def _():
-            ghost_sum(j).start()
+            ghost_sum(j, 0).start()
+            ghost_sum(j, 1).start()
     owned = nodes[0:OWN_ROWS]
     for c in range(1, 4):
         owned = owned + scatter(c, OWN_ROWS)
     owned = jnp.concatenate([owned[:, 0:128], owned[:, 128:256]], axis=0)
 
-    for j in range(4):
-        @pl.when(valid[j])
-        def _():
-            remote(gh_send.at[j], gh_recv.at[j], gh_s.at[j], gh_r.at[j], g, p + OFFSETS[j]).wait_recv()
-    row64 = iota((64, 128), 0)
-    added = None
-    for d in range(4):
-        ids = shared[d : d + 1, :]
-        high, low = split_bf16(gh_recv[d])
-        spread = jnp.where((row64 & 31) == (ids >> 7), jnp.where(row64 < 32, high, low), 0.0).astype(bf16)
-        part = lax.dot_general(spread, one_hot(ids & 127, 128), (((1,), (1,)), ((), ())), preferred_element_type=f32)
-        added = part if added is None else added + part
-    owned = owned + (added[0:32] + added[32:64])
-
-    core, chip, chips = lax.rem(g, 2), g // 2, layers // 2
-    mate = g + 1 - 2 * core
     pair_send[0] = owned[0:16]
     pair_send[1] = owned[16:32]
     pair = remote(pair_send.at[1 - core], pair_recv, pair_s, pair_r, mate, p)
     pair.start()
+
+    line32 = iota((32, 512), 0)
+    ids = jnp.concatenate([shared[d : d + 1, :] for d in range(4)], axis=1)
+    hots = one_hot(ids & 127, 128)
+    spots = (line32 & 15) + 16 * core == (ids >> 7)
     pair.wait_recv()
-    all_recv[chip] = pair_send[core] + pair_recv[...]
+    for j in range(4):
+        @pl.when(valid[j])
+        def _():
+            ghost_from(j, 0).wait_recv()
+            ghost_from(j, 1).wait_recv()
+
+    high, low = split_bf16(jnp.concatenate([gh_recv[0, d] + gh_recv[1, d] for d in range(4)], axis=1))
+    spread = jnp.where(spots, jnp.where(line32 < 16, high, low), 0.0).astype(bf16)
+    added = lax.dot_general(spread, hots, (((1,), (1,)), ((), ())), preferred_element_type=f32)
+    all_recv[chip] = (pair_send[core] + pair_recv[...]) + (added[0:16] + added[16:32])
 
     def over_chips(k):
         i = lax.rem(chip + k, chips)
@@ -462,7 +469,8 @@
         @pl.when(valid[j])
         def _():
             ghost(j).wait_send()
-            ghost_sum(j).wait_send()
+            ghost_sum(j, 0).wait_send()
+            ghost_sum(j, 1).wait_send()
 
         @pl.when(jnp.logical_and(valid[j], up))
         def _():
@@ -516,11 +524,11 @@
             vmem((layers, 2 * per, WIDE), f32), vmem((layers, 2 * per, WIDE), f32),
             vmem((layers, per, WIDE), f32), vmem((layers, per, WIDE), f32),
             vmem((1, elems), f32), vmem((1, elems), f32),
-            vmem((4, 1, 128), f32), vmem((4, 1, 128), f32),
+            vmem((4, 1, 128), f32), vmem((2, 4, 1, 128), f32),
             vmem((2, 16, 128), f32), vmem((16, 128), f32), vmem((layers // 2, 16, 128), f32), vmem((2, 16, 128), f32),
             dma((10,)), dma, dma, dma((3,)), dma((3,)), dma((4,)), dma((4,)), dma((4,)), dma((4,)),
         ]
-        + [dma((layers,)), dma((layers,)), dma((layers,)), dma((layers,)), dma((4,)), dma((4,)), dma, dma]
+        + [dma((layers,)), dma((layers,)), dma((layers,)), dma((layers,)), dma((2, 4)), dma((2, 4)), dma, dma]
         + [dma((layers // 2,)), dma((layers // 2,)), dma, dma],
         compiler_params=pltpu.CompilerParams(collective_id=0, has_side_effects=True, vmem_limit_bytes=60 << 20),
         name="ice_gradient",

time: 38.8 us -> 38 us (0.979)
  Pallas kernels: 37 us -> 36.4 us
    pallas_call x1, Pallas kernels: 37 us -> 36.4 us  [shards(): pl.pallas_call(functools.partial(kernel, layers, planes), out_shape=jax.S...]
where the time goes in v5:
time: 38 us; the launch traced here: 37.7 us
  Pallas kernels  36.4 us (96%)
  local copies, waits for them, and re-layouts  1.32 us (3%)
    pallas_call x1, Pallas kernels, shards(): pl.pallas_call(functools.partial(kernel, layers, planes), out_shape=jax.S...  36.4 us
    unnamed x1, local copies, waits for them, and re-layouts  1.32 us

profile of v5, /device:TPU:7, one launch (start us, length us, event | category | flops | bytes accessed | tf_op | source)
XLA Modules:
  0.0 37.7 jit_solution(5206623773147684399)
XLA Ops:
  0.0 36.4 %ice_gradient.1 = f32[32,128]{1,0:T(8,128)} custom-call(bf16[2,8,4096]{2,1,0:T(8,128)(2,1)} %vel_hbm.1, bf16[2,8,4096]{2,1,0:T(8,128)(2,1)} %adj_hbm.1, s32[4,4096]{1,0:T(4,128)} %cor_hbm.1, s32[4,128]{1,0:T(4,128)} %sha_hbm.1, f32[2,4096]{1,0:T(2,128)} %str_hbm.1, f32[2,4096]{1,0:T(2,128)} %she_hbm.1, f32[8,4096]{1,0:T(8,128)} %thi_hbm.1, ...), custom_call_target="tpu_custom_call" | custom-call | tf_op jit(solution)/shard_map/ice_gradient/pallas_call | solution.py:510
  36.4 1.3 %copy.12 = f32[4096]{0:T(1024)} copy(f32[4096]{0:T(1024)} %bitcast.1) | data formatting | bytes 32768

commit v6 on v5

--- a/solution.py
+++ b/solution.py
@@ -507,6 +507,7 @@
     elems = corners.shape[1]
     f32, bf16 = jnp.float32, jnp.bfloat16
     vmem, dma = pltpu.VMEM, pltpu.SemaphoreType.DMA
+    args = [pltpu.with_memory_space_constraint(x, pltpu.HBM) for x in args]
     out = pl.pallas_call(
         functools.partial(kernel, layers, planes),
         out_shape=jax.ShapeDtypeStruct((32, 128), f32),
@@ -530,7 +531,7 @@
         ]
         + [dma((layers,)), dma((layers,)), dma((layers,)), dma((layers,)), dma((2, 4)), dma((2, 4)), dma, dma]
         + [dma((layers // 2,)), dma((layers // 2,)), dma, dma],
-        compiler_params=pltpu.CompilerParams(collective_id=0, has_side_effects=True, vmem_limit_bytes=60 << 20),
+        compiler_params=pltpu.CompilerParams(collective_id=0, has_side_effects=True, vmem_limit_bytes=40 << 20),
         name="ice_gradient",
     )(*args)
     return out.reshape(4096)

time: 38 us -> 36.6 us (0.963)
  local copies, waits for them, and re-layouts: 1.32 us -> 0.61 us
  Pallas kernels: 36.4 us -> 35.8 us
    unnamed x1, local copies, waits for them, and re-layouts: 1.32 us -> 0.61 us
    pallas_call x1, Pallas kernels: 36.4 us -> 35.8 us  [shards(): pl.pallas_call(functools.partial(kernel, layers, planes), out_shape=jax.S...]
where the time goes in v6:
time: 36.6 us; the launch traced here: 36.4 us
  Pallas kernels  35.8 us (98%)
  local copies, waits for them, and re-layouts  0.61 us (2%)
    pallas_call x1, Pallas kernels, shards(): pl.pallas_call(functools.partial(kernel, layers, planes), out_shape=jax.S...  35.8 us

profile of v6, /device:TPU:7, one launch (start us, length us, event | category | flops | bytes accessed | tf_op | source)
XLA Modules:
  0.0 36.4 jit_solution(1932935812454689234)
XLA Ops:
  0.0 35.8 %ice_gradient.1 = f32[32,128]{1,0:T(8,128)S(1)} custom-call(bf16[2,8,4096]{2,1,0:T(8,128)(2,1)} %vel_hbm.1, bf16[2,8,4096]{2,1,0:T(8,128)(2,1)} %adj_hbm.1, s32[4,4096]{1,0:T(4,128)} %cor_hbm.1, s32[4,128]{1,0:T(4,128)} %sha_hbm.1, f32[2,4096]{1,0:T(2,128)} %str_hbm.1, f32[2,4096]{1,0:T(2,128)} %she_hbm.1, f32[8,4096]{1,0:T(8,128)} %thi_hbm.1, ...), custom_call_target="tpu_custom_call" | custom-call | tf_op jit(solution)/shard_map/ice_gradient/pallas_call | solution.py:511
  35.8 0.6 %copy.12 = f32[4096]{0:T(1024)} copy(f32[4096]{0:T(1024)S(1)} %bitcast.1) | data formatting | bytes 32768

commit v7 on v6

--- a/solution.py
+++ b/solution.py
@@ -143,7 +143,7 @@
     vel_hbm, adj_hbm, cor_hbm, sha_hbm, str_hbm, she_hbm, thi_hbm, rat_hbm, ret_hbm, wei_hbm,
     out,
     vel, adj, corners, shared, stretch, shear, thick, rate, ret, wei,
-    table, late, late8, hot, held, rows, low0, top_send, top_recv, low_send, low_own, gsend, grecv, lsend, lrecv,
+    table, late, hot, held, rows, low0, top_send, top_recv, low_send, low_own, gsend, grecv, lsend, lrecv,
     fac, off, sc_send, sc_recv, en_send, en_recv,
     abuf, bbuf,
     gh_send, gh_recv, pair_send, pair_recv, all_recv, done,
@@ -351,16 +351,16 @@
 
     for i in range(2):
         late[i * 32 : (i + 1) * 32] = jnp.concatenate([grecv[2 * i], grecv[2 * i + 1]], axis=1)
-    late8[0:64] = low_own[...]
+    late[64:128] = low_own[...]
     first = jnp.concatenate([lrecv[0], lrecv[1]], axis=1).astype(f32)[0:8]
     second = jnp.concatenate([lrecv[2], lrecv[3]], axis=1).astype(f32)[0:8]
     ghosts8 = first + pltpu.roll(second, 4, 0)
-    late8[64:80] = jnp.concatenate([ghosts8, jnp.zeros((8, WIDE), f32)], axis=0).astype(bf16)
+    late[128:144] = jnp.concatenate([ghosts8, jnp.zeros((8, WIDE), f32)], axis=0).astype(bf16)
 
     row = rows[0:1, :]
     found = jnp.dot(late[...], hot[0], preferred_element_type=f32)
     held[0] = jnp.where(row == 17, found[32:64], jnp.where(row == 16, found[0:32], held[0]))
-    both = pick(row >> 1, 8, jnp.dot(late8[...], hot[0], preferred_element_type=f32), ALL_ROWS // 2)
+    both = pick(row >> 1, 8, found[64:136], ALL_ROWS // 2)
     low0[...] = jnp.where((row & 1) == 1, pltpu.roll(both, 4, 0), both)
 
     for i in range(3):
@@ -515,7 +515,7 @@
         out_specs=pl.BlockSpec(memory_space=pltpu.VMEM),
         scratch_shapes=[vmem(a.shape, a.dtype) for a in args]
         + [
-            vmem((OWN_ROWS * 32, WIDE), bf16), vmem((64, WIDE), bf16), vmem((80, WIDE), bf16),
+            vmem((OWN_ROWS * 32, WIDE), bf16), vmem((144, WIDE), bf16),
             vmem((4, WIDE, elems), bf16), vmem((4, 32, elems), f32), vmem((4, elems), jnp.int32), vmem((8, elems), f32),
             vmem((3, 4, elems), bf16), vmem((3, 4, elems), bf16),
             vmem((64, WIDE), bf16), vmem((64, WIDE), bf16),

time: 36.6 us -> 36.2 us (0.989)
  Pallas kernels: 35.8 us -> 35.4 us
    pallas_call x1, Pallas kernels: 35.8 us -> 35.4 us  [shards(): pl.pallas_call(functools.partial(kernel, layers, planes), out_shape=jax.S...]
where the time goes in v7:
time: 36.2 us; the launch traced here: 36 us
  Pallas kernels  35.4 us (98%)
  local copies, waits for them, and re-layouts  0.61 us (2%)
    pallas_call x1, Pallas kernels, shards(): pl.pallas_call(functools.partial(kernel, layers, planes), out_shape=jax.S...  35.4 us

profile of v7, /device:TPU:7, one launch (start us, length us, event | category | flops | bytes accessed | tf_op | source)
XLA Modules:
  0.0 36.0 jit_solution(16474453915806361812)
XLA Ops:
  0.0 35.4 %ice_gradient.1 = f32[32,128]{1,0:T(8,128)S(1)} custom-call(bf16[2,8,4096]{2,1,0:T(8,128)(2,1)} %vel_hbm.1, bf16[2,8,4096]{2,1,0:T(8,128)(2,1)} %adj_hbm.1, s32[4,4096]{1,0:T(4,128)} %cor_hbm.1, s32[4,128]{1,0:T(4,128)} %sha_hbm.1, f32[2,4096]{1,0:T(2,128)} %str_hbm.1, f32[2,4096]{1,0:T(2,128)} %she_hbm.1, f32[8,4096]{1,0:T(8,128)} %thi_hbm.1, ...), custom_call_target="tpu_custom_call" | custom-call | tf_op jit(solution)/shard_map/ice_gradient/pallas_call | solution.py:511
  35.4 0.6 %copy.12 = f32[4096]{0:T(1024)} copy(f32[4096]{0:T(1024)S(1)} %bitcast.1) | data formatting | bytes 32768

commit v8 on v7

--- a/solution.py
+++ b/solution.py
@@ -16,7 +16,7 @@
 HALF = 2048
 OWN_ROWS = 16
 ALL_ROWS = 18
-MAIN_BLOCK = 512
+MAIN_BLOCK = 256
 SCATTER_BLOCK = 4096
 
 
@@ -388,8 +388,8 @@
             at = slice((i * per + k) * WIDE, (i * per + k + 1) * WIDE)
             abuf[:, at] = 0.25 * (abuf[:, at] * en_recv[i, k : k + 1, :] + bbuf[:, at])
 
-    def scatter(c, count):
-        def block(b, total):
+    def scatter(which, count):
+        def block(b, c, total):
             at = slice(b * SCATTER_BLOCK, (b + 1) * SCATTER_BLOCK)
             line = iota((2 * count, SCATTER_BLOCK), 0)
             high, low = split_bf16(abuf[:, at])
@@ -398,7 +398,10 @@
             spread = jnp.where(place == rows[c : c + 1, at], value, 0.0).astype(bf16)
             return total + lax.dot_general(hot[c, :, at], spread, (((1,), (1,)), ((), ())), preferred_element_type=f32)
 
-        total = block(0, jnp.zeros((WIDE, 2 * count), f32)).T
+        total = jnp.zeros((WIDE, 2 * count), f32)
+        for c in which:
+            total = block(0, c, total)
+        total = total.T
         return total[0:count] + total[count : 2 * count]
 
     core, chip, chips = lax.rem(g, 2), g // 2, layers // 2
@@ -411,7 +414,7 @@
     def ghost_from(j, k):
         return remote(gh_send.at[j], gh_recv.at[k, j], gh_s.at[0, j], gh_r.at[k, j], g, p + OFFSETS[j])
 
-    nodes = scatter(0, 24)
+    nodes = scatter((0,), 24)
     for j in range(4):
         gh_send[j] = nodes[OWN_ROWS + j // 2 : OWN_ROWS + j // 2 + 1, (j % 2) * 128 : (j % 2 + 1) * 128]
     for j in range(4):
@@ -419,9 +422,7 @@
         def _():
             ghost_sum(j, 0).start()
             ghost_sum(j, 1).start()
-    owned = nodes[0:OWN_ROWS]
-    for c in range(1, 4):
-        owned = owned + scatter(c, OWN_ROWS)
+    owned = nodes[0:OWN_ROWS] + scatter((1, 2, 3), OWN_ROWS)
     owned = jnp.concatenate([owned[:, 0:128], owned[:, 128:256]], axis=0)
 
     pair_send[0] = owned[0:16]

time: 36.2 us -> 36.2 us (level)
  no operation moved by 1% of the time
where the time goes in v8:
time: 36.2 us; the launch traced here: 36 us
  Pallas kernels  35.4 us (98%)
  local copies, waits for them, and re-layouts  0.61 us (2%)
    pallas_call x1, Pallas kernels, shards(): pl.pallas_call(functools.partial(kernel, layers, planes), out_shape=jax.S...  35.4 us

profile of v8, /device:TPU:7, one launch (start us, length us, event | category | flops | bytes accessed | tf_op | source)
XLA Modules:
  0.0 36.0 jit_solution(16131116263776702682)
XLA Ops:
  0.0 35.4 %ice_gradient.1 = f32[32,128]{1,0:T(8,128)S(1)} custom-call(bf16[2,8,4096]{2,1,0:T(8,128)(2,1)} %vel_hbm.1, bf16[2,8,4096]{2,1,0:T(8,128)(2,1)} %adj_hbm.1, s32[4,4096]{1,0:T(4,128)} %cor_hbm.1, s32[4,128]{1,0:T(4,128)} %sha_hbm.1, f32[2,4096]{1,0:T(2,128)} %str_hbm.1, f32[2,4096]{1,0:T(2,128)} %she_hbm.1, f32[8,4096]{1,0:T(8,128)} %thi_hbm.1, ...), custom_call_target="tpu_custom_call" | custom-call | tf_op jit(solution)/shard_map/ice_gradient/pallas_call | solution.py:512
  35.4 0.6 %copy.12 = f32[4096]{0:T(1024)} copy(f32[4096]{0:T(1024)S(1)} %bitcast.1) | data formatting | bytes 32768
